TPU v7x, 32 devices: a whole 2x2x4 slice. The times are simulated.
32 devices in a mesh: dp: 4 (over y, x), seq: 8 (over z, core).
Axes of the slice: x: 2, y: 2, z: 4, core: 2. Of those that a mesh axis runs over, the one named last changes fastest.
Arguments:
- tokens: bfloat16 [8, 512, 1024], P('dp', 'seq'), may hold values from -6 to 6
- memory: bfloat16 [8, 512, 1024], P('dp', 'seq'), may hold values from -6 to 6
- cotangent: bfloat16 [8, 512, 1024], P('dp', 'seq'), may hold values from -6 to 6
- block_ids: int32 [8, 512], P('dp'), may hold values from 0 to 3, never falling along the last dimension, each value on 1 to 256 neighbouring positions
- seq_lengths: int32 [8], P('dp'), may hold values from 256 to 512, as said below
- self_query: bfloat16 [1024, 1024], P(('dp', 'seq')), may hold values from -0.1875 to 0.1875
- self_key: bfloat16 [1024, 1024], P(('dp', 'seq')), may hold values from -0.1875 to 0.1875
- self_value: bfloat16 [1024, 1024], P(('dp', 'seq')), may hold values from -0.1875 to 0.1875
- self_out: bfloat16 [1024, 1024], P(('dp', 'seq')), may hold values from -3 to 3
- cross_query: bfloat16 [1024, 1024], P(('dp', 'seq')), may hold values from -0.1875 to 0.1875
- cross_key: bfloat16 [1024, 1024], P(('dp', 'seq')), may hold values from -0.1875 to 0.1875
- cross_value: bfloat16 [1024, 1024], P(('dp', 'seq')), may hold values from -0.1875 to 0.1875
- cross_out: bfloat16 [1024, 1024], P(('dp', 'seq')), may hold values from -3 to 3
- ffn_up: bfloat16 [1024, 4096], P(('dp', 'seq')), may hold values from -0.1875 to 0.1875
- ffn_down: bfloat16 [4096, 1024], P(('dp', 'seq')), may hold values from -0.09375 to 0.09375
- attn_gain: bfloat16 [1024], P(('dp', 'seq')), may hold values from 0.25 to 1.75
- attn_bias: bfloat16 [1024], P(('dp', 'seq')), may hold values from -3 to 3
- cross_gain: bfloat16 [1024], P(('dp', 'seq')), may hold values from 0.25 to 1.75
- cross_bias: bfloat16 [1024], P(('dp', 'seq')), may hold values from -3 to 3
- feedforward_norm_gain: bfloat16 [1024], P(('dp', 'seq')), may hold values from 0.25 to 1.75
- ffn_bias: bfloat16 [1024], P(('dp', 'seq')), may hold values from -3 to 3
Outputs:
- layer_out: bfloat16 [8, 512, 1024], P('dp', 'seq')
- tokens_grad: bfloat16 [8, 512, 1024], P('dp', 'seq')
- memory_grad: bfloat16 [8, 512, 1024], P('dp', 'seq')
- self_query_grad: float32 [1024, 1024], P(('dp', 'seq'))
- self_key_grad: float32 [1024, 1024], P(('dp', 'seq'))
- self_value_grad: float32 [1024, 1024], P(('dp', 'seq'))
- self_out_grad: float32 [1024, 1024], P(('dp', 'seq'))
- cross_query_grad: float32 [1024, 1024], P(('dp', 'seq'))
- cross_key_grad: float32 [1024, 1024], P(('dp', 'seq'))
- cross_value_grad: float32 [1024, 1024], P(('dp', 'seq'))
- cross_out_grad: float32 [1024, 1024], P(('dp', 'seq'))
- ffn_up_grad: float32 [1024, 4096], P(('dp', 'seq'))
- ffn_down_grad: float32 [4096, 1024], P(('dp', 'seq'))
- attn_gain_grad: float32 [1024], P(('dp', 'seq'))
- attn_bias_grad: float32 [1024], P(('dp', 'seq'))
- cross_gain_grad: float32 [1024], P(('dp', 'seq'))
- cross_bias_grad: float32 [1024], P(('dp', 'seq'))
- ffn_gain_grad: float32 [1024], P(('dp', 'seq'))
- ffn_bias_grad: float32 [1024], P(('dp', 'seq'))
Inputs may be any that keep to these rules, and one draw needn't show every extreme that they name: `seq_lengths`: some sequence in every draw has all 512 tokens live. `block_ids`: along each sequence the block ids never fall, and each block spans 1 to 256 positions, some block exactly 256.
All inputs are finite; a program needn't handle non-finite values.
Results may differ from a plain program's by a relative error of at most 0.025.
Values may be sent and summed in bfloat16 or wider, within the bound.
No kernel may reach another device: no remote copies, remote signals or barrier semaphores. Data moves between devices by JAX's collectives and lax.ppermute only.
A program may use at most 192 MiB of HBM per device.

v0:
```python
import jax
import jax.numpy as jnp
from jax import lax
from jax.experimental import pallas as pl
from jax.experimental.pallas import tpu as pltpu
from jax.sharding import Mesh, PartitionSpec as P

HEAD_DIM = 64
CORES = 2

eps_norm = 1e-05
residual_scale = 18.0**0.25
gelu_coef = 0.7978845608028654
neg_large = -1e30
bf16 = jnp.bfloat16
f32 = jnp.float32


def gelu_tanh(values_in):
    inner = gelu_coef * (values_in + 0.044715 * values_in * values_in * values_in)
    return 0.5 * values_in * (1.0 + jnp.tanh(inner))


def gelu_slope(values_in):
    squared = values_in * values_in
    tanh_val = jnp.tanh(gelu_coef * (values_in + 0.044715 * squared * values_in))
    return 0.5 * (1.0 + tanh_val) + 0.5 * values_in * (1.0 - tanh_val * tanh_val) * gelu_coef * (
        1.0 + 3.0 * 0.044715 * squared
    )


def matmul(first_mat, second_mat):
    return jnp.dot(first_mat, second_mat, preferred_element_type=f32)


def transposed_product(first_mat, second_mat):
    return lax.dot_general(first_mat, second_mat, (((1,), (1,)), ((), ())), preferred_element_type=f32)


def outer_product_sum(first_mat, second_mat):
    return lax.dot_general(first_mat, second_mat, (((0,), (0,)), ((), ())), preferred_element_type=f32)


LIMIT = pltpu.CompilerParams(vmem_limit_bytes=16 * 1024 * 1024)
ALL_OF_IT = pltpu.CompilerParams(vmem_limit_bytes=60 * 1024 * 1024)
SCALAR = pl.BlockSpec(memory_space=pltpu.SMEM)
WHOLE = pl.BlockSpec(memory_space=pltpu.VMEM)


def on_chip(values):
    return pltpu.with_memory_space_constraint(values, pltpu.VMEM)


def chip_call(kernel, outs, name, *args, scalar=None):
    scalars = [] if scalar is None else [scalar.reshape(1)]
    return pl.pallas_call(
        kernel,
        in_specs=[SCALAR] * len(scalars) + [WHOLE] * len(args),
        out_specs=[WHOLE] * len(outs),
        out_shape=[pltpu.VMEM(shape, dtype) for shape, dtype in outs],
        compiler_params=LIMIT,
        name=name,
    )(*scalars, *[on_chip(x) for x in args])


ANY = pl.BlockSpec(memory_space=pl.ANY)
FAR = pl.BlockSpec(memory_space=pltpu.HBM)


def copy_call(copies, out, name, scalar, *args):
    count = []

    def kernel(scalar_ref, *refs):
        sems = refs[-1]
        running = [
            pltpu.make_async_copy(source, target, sems.at[i])
            for i, (source, target) in enumerate(copies(scalar_ref[0], refs[:-2], refs[-2]))
        ]
        for one in running:
            one.start()
        for one in running:
            one.wait()

    class Probe:
        at = property(lambda self: self)

        def __getitem__(self, index):
            return self

    count = len(copies(0, [Probe()] * len(args), Probe()))
    return pl.pallas_call(
        kernel,
        in_specs=[SCALAR] + [ANY] * len(args),
        out_specs=ANY,
        out_shape=jax.ShapeDtypeStruct(*out),
        scratch_shapes=[pltpu.SemaphoreType.DMA((count,))],
        compiler_params=LIMIT,
        name=name,
    )(scalar.reshape(1), *args)


def _mean(values):
    return jnp.mean(values, axis=-1, keepdims=True)


def _normed(residual, kept, came):
    values = residual_scale * residual.astype(f32) + (kept + came.astype(f32))
    centred = values - _mean(values)
    inv_std = lax.rsqrt(_mean(centred * centred) + eps_norm)
    return centred * inv_std, inv_std


def _norm_back(grad_out, normed, inv_std, gain):
    scaled = grad_out * gain
    grad_in = inv_std * (scaled - _mean(scaled) - normed * _mean(scaled * normed))
    sums = [jnp.sum(grad_out * normed, axis=0, keepdims=True), jnp.sum(grad_out, axis=0, keepdims=True)]
    return grad_in, jnp.concatenate(sums, axis=0)


def norm_rows(residual, kept, came, vectors, row):
    def kernel(res, kept, came, vec, hidden, normed, inv):
        n, r = _normed(res[...], kept[...], came[...])
        hidden[...] = (n * vec[row : row + 1, :] + vec[row + 1 : row + 2, :]).astype(bf16)
        normed[...] = n
        inv[...] = jnp.broadcast_to(r, inv.shape)

    shape = residual.shape
    outs = [(shape, bf16), (shape, f32), ((shape[0], 128), f32)]
    return chip_call(kernel, outs, "norm_rows", residual, kept, came, vectors)


def norm_turn(residual, kept, came, vectors, row, cotangent):
    def kernel(res, kept, came, vec, cot, layer, grad, rounded, sums):
        gain = vec[row : row + 1, :]
        n, r = _normed(res[...], kept[...], came[...])
        layer[...] = (n * gain + vec[row + 1 : row + 2, :]).astype(bf16)
        g, s = _norm_back(cot[...].astype(f32), n, r, gain)
        grad[...] = g
        rounded[...] = g.astype(bf16)
        sums[...] = s

    shape = residual.shape
    outs = [(shape, bf16), (shape, f32), (shape, bf16), ((2, shape[1]), f32)]
    return chip_call(kernel, outs, "norm_turn", residual, kept, came, vectors, cotangent)


def norm_back(grad_prev, kept, came, normed, inv_std, vectors, row):
    shape = grad_prev.shape
    args = [grad_prev, kept, came, normed, inv_std]

    def kernel(*refs):
        vec, grad, rounded, sums = refs[5:9]
        prev, kept, came, normed, inv = refs[9:14]
        running = [pltpu.make_async_copy(refs[i], refs[9 + i], refs[14].at[i]) for i in range(5)]
        for one in running:
            one.start()
        for one in running:
            one.wait()
        grad_out = residual_scale * prev[...] + (kept[...] + came[...].astype(f32))
        g, s = _norm_back(grad_out, normed[...], inv[:, :1], vec[row : row + 1, :])
        grad[...] = g
        rounded[...] = g.astype(bf16)
        sums[...] = s

    outs = [(shape, f32), (shape, bf16), ((2, shape[1]), f32)]
    return pl.pallas_call(
        kernel,
        in_specs=[FAR] * 5 + [WHOLE],
        out_specs=[WHOLE] * 3,
        out_shape=[pltpu.VMEM(x, dtype) for x, dtype in outs],
        scratch_shapes=[pltpu.VMEM(x.shape, x.dtype) for x in args] + [pltpu.SemaphoreType.DMA((5,))],
        compiler_params=LIMIT,
        name="norm_back",
    )(*args, on_chip(vectors))


PAIR = 2 * HEAD_DIM


def _head_of_pair(values, head):
    lane = lax.broadcasted_iota(jnp.int32, (1, PAIR), 1)
    return jnp.where((lane // HEAD_DIM) == head, values, jnp.zeros((), values.dtype))


def _times(first, second, dims):
    return lax.dot_general(first, second, ((dims[:1], dims[1:]), ((), ())), preferred_element_type=f32)


def attention_forward(queries, keys, values, bias):
    rows, width = queries.shape
    key_rows = keys.shape[0]
    scale = HEAD_DIM ** (-0.5)

    def kernel(q_ref, k_ref, v_ref, *rest):
        out_ref, probs_ref = rest[-2:]
        for pair in range(width // PAIR):
            cols = slice(pair * PAIR, (pair + 1) * PAIR)
            q, k, v = q_ref[:, cols] * jnp.asarray(scale, bf16), k_ref[:, cols], v_ref[:, cols]
            mixed = None
            for head in range(2):
                scores = _times(k, _head_of_pair(q, head), (1, 1))
                if bias is not None:
                    scores = scores + rest[0][...]
                expo = jnp.exp(scores - jnp.max(scores, axis=0, keepdims=True))
                probs = (expo * (1.0 / jnp.sum(expo, axis=0, keepdims=True))).astype(bf16)
                probs_ref[2 * pair + head] = probs
                part = _times(_head_of_pair(v, head), probs, (0, 0))
                mixed = part if mixed is None else mixed + part
            out_ref[:, cols] = mixed.T.astype(bf16)

    args = [queries, keys, values] + ([] if bias is None else [bias])
    outs = [((rows, width), bf16), ((width // HEAD_DIM, key_rows, rows), bf16)]
    return chip_call(kernel, outs, "attend", *args)


def attention_backward(queries, keys, values, probs, first, grad_mixed, sums, last):
    rows, width = queries.shape
    key_rows = keys.shape[0]
    scale = HEAD_DIM ** (-0.5)

    def kernel(q_ref, k_ref, v_ref, p_ref, g_ref, *rest):
        before, (dq_ref, dk_ref, dv_ref) = rest[: len(sums)], rest[len(sums) :]
        for pair in range(width // PAIR):
            cols = slice(pair * PAIR, (pair + 1) * PAIR)
            q, k, v, g = q_ref[:, cols], k_ref[:, cols], v_ref[:, cols], g_ref[:, cols]
            dq = None
            dk, dv = [x[:, cols] for x in before] if sums else (None, None)
            for head in range(2):
                g_one = _head_of_pair(g, head)
                rounded = p_ref[2 * pair + head, :, first : first + rows]
                wide = rounded.astype(f32)
                weighted = _times(v, g_one, (1, 1)) * wide
                g_scores = (weighted - wide * jnp.sum(weighted, axis=0, keepdims=True)).astype(bf16)
                part_q = _times(_head_of_pair(k, head), g_scores, (0, 0))
                part_k = _times(g_scores, _head_of_pair(q, head), (1, 0))
                part_v = _times(rounded, g_one, (1, 0))
                dq = part_q if dq is None else dq + part_q
                dk = part_k if dk is None else dk + part_k
                dv = part_v if dv is None else dv + part_v
            dq_ref[:, cols] = (dq.T * scale).astype(bf16)
            dk_ref[:, cols] = (dk * scale).astype(bf16) if last else dk
            dv_ref[:, cols] = dv.astype(dv_ref.dtype)

    kind = bf16 if last else f32
    outs = [((rows, width), bf16), ((key_rows, width), kind), ((key_rows, width), kind)]
    return chip_call(kernel, outs, "attend_back", queries, keys, values, probs, grad_mixed, *sums)


def swap(values, name, size, flip):
    return lax.ppermute(values, name, [(i, i ^ flip) for i in range(size)])


def flip_bits(size):
    return [1 << b for b in range(size.bit_length() - 1)]


sync = lambda *values: lax.optimization_barrier(values)


def tie(value, *others):
    return lax.optimization_barrier((value,) + others)[0]


def lay_out(ranks, query, key, value, mem_key, mem_value, cross, up, own_out, mem_out):
    rows, width = query.shape
    part = width // ranks
    ff_part = up.shape[1] // ranks
    groups = ff_part * ranks // up.shape[1] * (width // (ranks * rows))
    unit = ff_part // groups

    def kernel(*refs):
        (self_ref, cross_ref, up_ref, so_ref, co_ref), ins, sems = refs[9:14], refs[14:23], refs[23]
        running = [pltpu.make_async_copy(refs[i], ins[i], sems.at[i]) for i in range(9)]
        for one in running:
            one.start()
        for one in running:
            one.wait()
        for r in range(ranks):
            cols = slice(r * part, (r + 1) * part)
            for i in range(3):
                self_ref[r, :, i * part : (i + 1) * part] = ins[i][:, cols]
                cross_ref[r, :, i * part : (i + 1) * part] = ins[3 + i][:, cols]
            so_ref[r] = ins[7][:, cols]
            co_ref[r] = ins[8][:, cols]
            for g in range(groups):
                first = (g * ranks + r) * unit
                up_ref[r, :, g * unit : (g + 1) * unit] = ins[6][:, first : first + unit]

    shapes = [3 * part, 3 * part, ff_part, part, part]
    return pl.pallas_call(
        kernel,
        in_specs=[FAR] * 9,
        out_specs=[WHOLE] * 5,
        scratch_shapes=[pltpu.VMEM((rows, width), bf16)] * 6
        + [pltpu.VMEM(up.shape, bf16)]
        + [pltpu.VMEM((rows, width), bf16)] * 2
        + [pltpu.SemaphoreType.DMA((9,))],
        out_shape=[pltpu.VMEM((ranks, rows, n), bf16) for n in shapes],
        compiler_params=ALL_OF_IT,
        name="lay_out",
    )(query, key, value, mem_key, mem_value, cross, up, own_out, mem_out)


def columns_back(pieces, counts, unit_first):
    ranks, rows, _ = pieces.shape

    def kernel(in_ref, *outs):
        first = 0
        for out, count in zip(outs, counts):
            if out is outs[0] and unit_first:
                units = count // unit_first
                for r in range(ranks):
                    for g in range(units):
                        at = (g * ranks + r) * unit_first
                        out[:, at : at + unit_first] = in_ref[
                            r, :, first + g * unit_first : first + (g + 1) * unit_first
                        ].astype(f32)
            else:
                for r in range(ranks):
                    out[:, r * count : (r + 1) * count] = in_ref[r, :, first : first + count].astype(f32)
            first += count

    return pl.pallas_call(
        kernel,
        in_specs=[WHOLE],
        out_specs=[WHOLE] * len(counts),
        out_shape=[jax.ShapeDtypeStruct((rows, ranks * n), f32) for n in counts],
        compiler_params=LIMIT,
        name="columns_back",
    )(on_chip(pieces))


def join_rows(pieces, rank):
    ranks = len(pieces)
    sets, blocks, rows, part = pieces[0].shape

    def copies(own, refs, out):
        return [
            (refs[r].at[p, b], out.at[p, own ^ r, :, b * part : (b + 1) * part])
            for r in range(ranks)
            for p in range(sets)
            for b in range(blocks)
        ]

    joined = copy_call(copies, ((sets, ranks, rows, blocks * part), bf16), "join_rows", rank, *pieces)
    return joined.reshape(sets * ranks * rows, blocks * part)


def pack_grads(rank, *parts):
    args = []
    places = []
    first = 0
    for one in parts:
        if isinstance(one, list):
            ranks, (sets, rows, width) = len(one), one[0].shape
            part = width // ranks
            for r in range(ranks):
                for p in range(sets):
                    for b in range(ranks):
                        at = slice(b * rows, (b + 1) * rows), slice(first, first + part)
                        places.append((len(args) + r, (p, slice(None), slice(b * part, (b + 1) * part)), (r, sets, p), at))
            args += one
            first += part
        else:
            groups, n, m = one.shape
            places.append((len(args), (slice(None),) * 3, None, (slice(None), slice(first, first + m))))
            args.append(one)
            first += m

    def copies(own, refs, out):
        found = []
        for i, source, piece, at in places:
            lead = slice(None) if piece is None else (own ^ piece[0]) * piece[1] + piece[2]
            found.append((refs[i].at[source], out.at[(lead,) + at]))
        return found

    return copy_call(copies, ((groups, n, first), bf16), "pack_grads", rank, *args)


def make_body(dp_size, g_size, z_size):
    ranks = z_size * CORES
    groups = dp_size * g_size
    every = ("dp", "g", "z", "c")

    def body(
        tokens,
        memory,
        cotangent,
        block_ids,
        seq_lengths,
        self_query,
        self_key,
        self_value,
        self_out,
        cross_query,
        cross_key,
        cross_value,
        cross_out,
        ffn_up,
        ffn_down,
        attn_gain,
        attn_bias,
        cross_gain,
        cross_bias,
        feedforward_norm_gain,
        ffn_bias,
    ):
        dp_own = lax.axis_index("dp")
        g_own = lax.axis_index("g")
        rank_own = lax.axis_index("z") * CORES + lax.axis_index("c")
        piece_rows = tokens.shape[1]
        width = tokens.shape[2]
        weight_rows = self_query.shape[0]
        rank_rows = ranks * weight_rows
        part = width // ranks
        sets = groups // ranks
        ff_rows = ffn_down.shape[0]
        ff_part = groups * ff_rows
        ff_blocks = width // ff_part

        def bits_of(name, size, own):
            return [(name, size, f, (own // f) % 2) for f in reversed(flip_bits(size))]

        axes = bits_of("dp", dp_size, dp_own) + bits_of("g", g_size, g_own)
        n_dp = dp_size.bit_length() - 1
        g_axes = list(range(n_dp, len(axes)))
        order_a = list(reversed(range(n_dp)))
        order_b = list(range(n_dp))

        def gather_axes(values, dims, order, after=()):
            for ax in order:
                name, size, flip, bit = axes[ax]
                other = tie(swap(values, name, size, flip), *after)
                pos = len([d for d in dims if d < ax])
                values = jnp.where(
                    bit == 1, jnp.stack([other, values], pos), jnp.stack([values, other], pos)
                )
                dims = sorted(dims + [ax])
            return values

        def scatter_axes(values, dims, order):
            dims = list(dims)
            for i, ax in enumerate(order):
                name, size, flip, bit = axes[ax]
                pos = dims.index(ax)
                other = swap(
                    lax.dynamic_index_in_dim(values, 1 - bit, pos, keepdims=False), name, size, flip
                )
                kept = lax.dynamic_index_in_dim(values, bit, pos, keepdims=False)
                values = kept.astype(f32) + other.astype(f32)
                dims.remove(ax)
                if dims:
                    values = values.astype(bf16)
            return values

        def halves(n):
            return (2,) * n

        def finish(values):
            shape = values.shape[1:]
            return scatter_axes(values.reshape(halves(len(g_axes)) + shape), g_axes, g_axes)

        def rank_swap(values, flip):
            return swap(values, ("z", "c"), ranks, flip)

        def from_ranks(pieces, axis):
            got = []
            for f in range(ranks):
                piece = lax.dynamic_index_in_dim(pieces, rank_own ^ f, axis, keepdims=False)
                got.append(piece if f == 0 else rank_swap(piece, f))
            return got

        def gather_rows(values):
            return with_partner(gather_chips(values))

        def gather_chips(values):
            blocks = [values]
            for flip in flip_bits(z_size):
                blocks = blocks + [swap(b, "z", z_size, flip) for b in blocks]
            return blocks

        def with_partner(blocks):
            return [jnp.concatenate([b, swap(b, "c", CORES, 1)], axis=0) for b in blocks]

        def sum_rows(blocks, product, fill=None):
            own_rows = piece_rows * g_size
            sums = [None] * z_size
            for b in reversed(range(z_size)):
                partial = product(blocks[b])
                came = swap(partial[own_rows:].astype(bf16), "c", CORES, 1)
                sums[b] = partial[:own_rows] + came.astype(f32)
            for flip in reversed(flip_bits(z_size)):
                leaving = [sums[b + flip].astype(bf16) for b in range(flip)]
                came = [swap(x, "z", z_size, flip) for x in leaving]
                if flip > 1:
                    sums = [sums[b] + came[b].astype(f32) for b in range(flip)]
            if fill is None:
                return sums[0], came[0]
            filled = fill(leaving[0])
            kept, last, filled = lax.optimization_barrier((sums[0], came[0], filled))
            return kept, last, filled

        def bring_home(values):
            got = []
            for f in range(g_size):
                piece = lax.dynamic_index_in_dim(values, g_own ^ f, 0, keepdims=False)
                got.append(piece if f == 0 else swap(piece, "g", g_size, f))
            return jnp.concatenate(got, axis=-2)

        def send_back(values):
            blocks = values.reshape(g_size, piece_rows, width)
            got = [blocks[0]] + [swap(blocks[f], "g", g_size, f) for f in range(1, g_size)]
            got = jnp.stack(got)
            return jnp.stack(
                [lax.dynamic_index_in_dim(got, g_own ^ f, 0, keepdims=False) for f in range(g_size)]
            )

        own_tokens = bring_home(tokens)
        self_parts, cross_parts, up_parts, so_parts, co_parts = lay_out(
            ranks,
            self_query,
            self_key,
            self_value,
            cross_key,
            cross_value,
            cross_query,
            ffn_up,
            self_out,
            cross_out,
        )

        def to_ranks(parts_in):
            return lax.all_to_all(parts_in, ("z", "c"), 0, 0, tiled=True)

        self_own, own_tokens = sync(to_ranks(self_parts), own_tokens)
        self_set = jnp.concatenate([self_own, so_parts], axis=2).reshape(rank_rows, 4 * part)
        self_set = gather_axes(self_set, [], g_axes)
        token_blocks = gather_rows(own_tokens)
        other_own = to_ranks(tie(jnp.concatenate([cross_parts, up_parts], axis=2), self_own))
        half_a, half_b, *token_blocks = sync(
            self_set[..., : 2 * part], self_set[..., 2 * part :], *token_blocks
        )
        other_own = tie(other_own, half_a)

        first_a, rest_a = order_a[:1], order_a[1:]
        first_b, rest_b = order_b[:1], order_b[1:]

        def first_stage(pair):
            return [gather_axes(pair[0], g_axes, first_a), gather_axes(pair[1], g_axes, first_b)]

        def last_stage(pair):
            pair = [
                gather_axes(pair[0], sorted(g_axes + first_a), rest_a),
                gather_axes(pair[1], sorted(g_axes + first_b), rest_b),
            ]
            return [x.reshape((groups,) + x.shape[-2:]) for x in pair]

        assert len(g_axes) == 1
        g_axis = axes[g_axes[0]]

        def swap_groups(values):
            return swap(values, *g_axis[:3])

        def both_groups(own, other):
            return jnp.where(g_axis[3] == 1, jnp.stack([other, own]), jnp.stack([own, other]))

        self_pair = first_stage([half_a, half_b])
        cross_set = jnp.concatenate([other_own[..., : 3 * part], co_parts], axis=2)
        cross_set = cross_set.reshape(rank_rows, 4 * part)
        cross_other = swap_groups(cross_set)
        vectors = jnp.stack(
            [attn_gain, attn_bias, cross_gain, cross_bias, feedforward_norm_gain, ffn_bias]
        )
        vectors = jnp.broadcast_to(vectors[None], (groups * ranks,) + vectors.shape)
        vectors = lax.all_to_all(tie(vectors, self_pair[0]), every, 0, 0, tiled=True)
        vectors = vectors.transpose(1, 0, 2).reshape(6, width).astype(f32)
        own_memory = bring_home(tie(memory, self_set))
        all_tokens = jnp.concatenate(token_blocks, axis=0)
        self_pair = last_stage(self_pair)
        cross_other = tie(cross_other, *self_pair)
        w_qk = self_pair[0].reshape(width, 2 * part)
        w_v = self_pair[1][..., :part].reshape(width, part)
        cross_set = both_groups(cross_set, cross_other)
        cross_pair = first_stage([cross_set[..., : 2 * part], cross_set[..., 2 * part :]])
        memory_chips = gather_chips(own_memory)

        down_rows = ffn_down.reshape(ff_rows, ff_blocks, ff_part).transpose(1, 0, 2)
        up_own, down_own = sync(
            other_own[..., 3 * part :].reshape(rank_rows, ff_part),
            down_rows.reshape(rank_rows, ff_part),
            self_pair[0],
        )[:2]
        up_other = swap_groups(up_own)
        down_other = swap_groups(tie(down_own, up_other))

        def out_rows(rows_in):
            pieces = rows_in.reshape(ranks, sets, ranks, weight_rows, part)
            return join_rows(from_ranks(pieces, 0), rank_own)

        w_sout = out_rows(self_pair[1][..., part:])

        n_pieces = g_size * ranks
        seq_own = g_own * ranks + rank_own
        ids = lax.dynamic_index_in_dim(block_ids, g_own, 0, keepdims=False)
        length = lax.dynamic_index_in_dim(seq_lengths, g_own, 0, keepdims=False)
        live = jnp.arange(ids.shape[0], dtype=jnp.int32) < length
        both = jnp.stack([ids, jnp.where(live, ids, jnp.int32(2**30))]).reshape(2, n_pieces, piece_rows)
        for flip in flip_bits(n_pieces):
            turned = both.reshape(2, n_pieces // (2 * flip), 2, flip, piece_rows)
            turned = jnp.concatenate([turned[:, :, 1:], turned[:, :, :1]], axis=2).reshape(both.shape)
            both = jnp.where((seq_own & flip) != 0, turned, both)
        both = both.reshape(2, g_size, ranks, piece_rows).transpose(0, 2, 1, 3).reshape(2, -1)
        bias = jnp.where(both[1][:, None] <= both[0][None, :], 0.0, neg_large).astype(f32)

        def row_blocks(values):
            return jnp.split(values, z_size, axis=0)

        def joined(blocks):
            return jnp.concatenate(blocks, axis=0)

        qk = matmul(all_tokens, w_qk).astype(bf16)
        queries, keys = qk[:, :part], qk[:, part:]
        values = matmul(all_tokens, w_v).astype(bf16)
        attended, self_probs = attention_forward(queries, keys, values, bias)
        attended, cross_pair[0], cross_pair[1], up_other = sync(attended, *cross_pair, up_other)
        cross_pair = last_stage(cross_pair)
        kept, came, memory_blocks = sum_rows(
            row_blocks(attended),
            lambda x: matmul(x, w_sout),
            lambda term: with_partner([tie(x, term) for x in memory_chips]),
        )
        kept, came, down_other = sync(kept, came, down_other)
        hidden_one, normed_one, inv_one = norm_rows(own_tokens, kept, came, vectors, 0)
        ffn_pair = first_stage([both_groups(up_own, up_other), both_groups(down_own, down_other)])
        own_cotangent = bring_home(tie(cotangent, down_other))

        all_memory = joined(memory_blocks)
        w_ckv = cross_pair[0].reshape(width, 2 * part)
        w_cq = cross_pair[1][..., :part].reshape(width, part)
        w_cout = out_rows(cross_pair[1][..., part:])
        mem_kv = matmul(all_memory, w_ckv).astype(bf16)
        mem_keys, mem_values = mem_kv[:, :part], mem_kv[:, part:]

        one_blocks = gather_rows(hidden_one)
        one_blocks[-1], mem_keys, mem_values, w_cout, ffn_pair[0], ffn_pair[1] = sync(
            one_blocks[-1], mem_keys, mem_values, w_cout, *ffn_pair
        )
        ffn_pair = last_stage(ffn_pair)
        cross_rows = [matmul(x, w_cq).astype(bf16) for x in one_blocks]
        crossed = [attention_forward(x, mem_keys, mem_values, None) for x in cross_rows]
        cross_probs = [x[1] for x in crossed]
        crossed = [x[0] for x in crossed]
        kept, came = sum_rows(crossed, lambda x: matmul(x, w_cout))
        hidden_two, normed_two, inv_two = norm_rows(hidden_one, kept, came, vectors, 2)
        hidden_two, own_cotangent = sync(hidden_two, own_cotangent)
        two_blocks = gather_rows(hidden_two)
        w_up = ffn_pair[0].reshape(width, ff_part)
        w_down = ffn_pair[1].reshape(groups, ff_blocks, ff_rows, ff_part).transpose(0, 2, 1, 3)
        w_down = w_down.reshape(ff_part, width)
        upper_rows = [matmul(x, w_up) for x in two_blocks]
        active_rows = [gelu_tanh(x).astype(bf16) for x in upper_rows]
        kept, came, slopes = sum_rows(
            active_rows,
            lambda x: matmul(x, w_down),
            lambda term: [gelu_slope(tie(x, term)) for x in upper_rows],
        )
        layer_rows, grad_three, branch, sums_three = norm_turn(
            hidden_two, kept, came, vectors, 4, own_cotangent
        )

        branch_blocks = gather_rows(branch)
        grad_upper = [
            (transposed_product(x, w_down) * y).astype(bf16) for x, y in zip(branch_blocks, slopes)
        ]

        def ffn_gradients(term):
            rows, _ = lax.optimization_barrier((branch_blocks, term))
            down = outer_product_sum(joined(active_rows), joined(rows)).astype(bf16)
            down = down.reshape(groups, ff_rows, ff_blocks, ff_part).transpose(0, 2, 1, 3)
            up = outer_product_sum(joined(two_blocks), joined(grad_upper)).astype(bf16)
            return jnp.concatenate(
                [up.reshape(groups, rank_rows, ff_part), down.reshape(groups, rank_rows, ff_part)],
                axis=1,
            )

        kept, came, ffn_grads = sum_rows(
            grad_upper, lambda x: transposed_product(x, w_up), ffn_gradients
        )
        ffn_grads = lax.psum_scatter(
            ffn_grads.reshape(groups * 2 * rank_rows, ff_part), "dp", scatter_dimension=0, tiled=True
        )
        grad_two, branch, sums_two = norm_back(grad_three, kept, came, normed_two, inv_two, vectors, 2)
        layer_out = send_back(tie(layer_rows, branch))

        branch_blocks = gather_rows(branch)
        branch_blocks[-1], layer_out = sync(branch_blocks[-1], layer_out)
        grad_crossed = [transposed_product(x, w_cout).astype(bf16) for x in branch_blocks]
        grad_cross_rows, sums = [], []
        for b in range(z_size):
            grad_rows, *sums = attention_backward(
                cross_rows[b], mem_keys, mem_values, cross_probs[b], 0, grad_crossed[b], sums, b == z_size - 1
            )
            grad_cross_rows.append(grad_rows)
        grad_mem_kv = jnp.concatenate(sums, axis=1)

        def cout_gradient(term):
            rows, _ = lax.optimization_barrier((branch_blocks, term))
            return outer_product_sum(joined(crossed), joined(rows)).astype(bf16)

        kept, came, cout_grad = sum_rows(
            grad_cross_rows, lambda x: transposed_product(x, w_cq), cout_gradient
        )
        grad_one, branch, sums_one = norm_back(grad_two, kept, came, normed_one, inv_one, vectors, 0)
        branch_blocks = gather_rows(branch)
        cout_grad = tie(cout_grad, branch).reshape(sets, ranks, weight_rows, width)
        cout_pieces = from_ranks(cout_grad, 1)
        vec_sums = jnp.concatenate([sums_one, sums_two, sums_three], axis=0)
        for flip in flip_bits(dp_size):
            vec_sums = vec_sums + swap(vec_sums, "dp", dp_size, flip)
        branch_blocks[-1], vec_sums = sync(branch_blocks[-1], vec_sums)
        grad_mem_kv = tie(grad_mem_kv, branch)
        mem_kv_grad = outer_product_sum(all_memory, grad_mem_kv).astype(bf16)
        cross_grad = outer_product_sum(joined(one_blocks), joined(grad_cross_rows)).astype(bf16)
        all_dims = list(range(len(axes)))

        def first_sums(pair):
            pair = [x.reshape(halves(len(axes)) + x.shape[-2:]) for x in pair]
            return [scatter_axes(pair[0], all_dims, first_a), scatter_axes(pair[1], all_dims, first_b)]

        def more_sums(pair):
            return [
                scatter_axes(pair[0], [d for d in all_dims if d not in first_a], rest_a),
                scatter_axes(pair[1], [d for d in all_dims if d not in first_b], rest_b),
            ]

        def last_sums(pair):
            return [scatter_axes(x, g_axes, g_axes) for x in pair]

        grad_attended = [transposed_product(x, w_sout).astype(bf16) for x in branch_blocks]
        sout_grad = outer_product_sum(attended, joined(branch_blocks)).astype(bf16)
        sout_pieces = from_ranks(sout_grad.reshape(sets, ranks, weight_rows, width), 1)
        memory_kept, memory_came = sum_rows(
            row_blocks(grad_mem_kv), lambda x: transposed_product(x, w_ckv)
        )
        memory_rows = (memory_kept + memory_came.astype(f32)).astype(bf16)

        query_blocks = row_blocks(queries)
        chip_rows = queries.shape[0] // z_size
        grad_queries, sums = [], []
        for b in range(z_size):
            grad_rows, *sums = attention_backward(
                query_blocks[b],
                keys,
                values,
                self_probs,
                b * chip_rows,
                grad_attended[b],
                sums,
                b == z_size - 1,
            )
            grad_queries.append(grad_rows)
        grad_qk = jnp.concatenate([joined(grad_queries), sums[0]], axis=1)
        grad_values = sums[1]
        def by_group(grads):
            return grads.reshape(groups, rank_rows, -1)

        qk_grad = outer_product_sum(all_tokens, grad_qk).astype(bf16)
        grads_a = pack_grads(rank_own, by_group(qk_grad), by_group(mem_kv_grad))
        v_grad = outer_product_sum(all_tokens, grad_values).astype(bf16)
        grads_b = pack_grads(rank_own, by_group(v_grad), sout_pieces, by_group(cross_grad), cout_pieces)
        sums = first_sums([grads_a, grads_b])

        sent = (grads_a, grads_b)
        ffn_grads = tie(ffn_grads, *sent).reshape(g_size, 2, rank_rows, ff_part)
        up_grad = scatter_axes(ffn_grads[:, 0], g_axes, g_axes)
        down_grad = scatter_axes(ffn_grads[:, 1], g_axes, g_axes)
        row_pairs = zip(row_blocks(tie(grad_qk, *sent)), row_blocks(grad_values))
        kept, came = sum_rows(
            list(row_pairs),
            lambda x: transposed_product(x[0], w_qk) + transposed_product(x[1], w_v),
        )
        tokens_grad = (residual_scale * grad_one + (kept + came.astype(f32))).astype(bf16)
        memory_grad = send_back(tie(memory_rows, *sent))
        sums[0], sums[1], up_grad, down_grad, tokens_grad = sync(*sums, up_grad, down_grad, tokens_grad)

        sums = more_sums(sums)
        up_pieces = to_ranks(up_grad.astype(bf16).reshape(ranks, weight_rows, ff_part))
        tokens_grad = send_back(tokens_grad)
        vec_sums = tie(vec_sums, tokens_grad)
        for name, size in (("c", CORES), ("z", z_size), ("g", g_size)):
            for flip in flip_bits(size):
                vec_sums = vec_sums + swap(vec_sums, name, size, flip)
        sums = last_sums(sums)

        down_grad = down_grad.reshape(ff_blocks, ff_rows, ff_part).transpose(1, 0, 2)
        down_grad = down_grad.reshape(ff_rows, width)

        def own_rows_of(values):
            return values.reshape(ranks, weight_rows, part).transpose(1, 0, 2).reshape(weight_rows, width)

        (up_grad,) = columns_back(up_pieces, (ff_part,), ff_rows)
        pieces = [sums[0][:, : 2 * part], sums[1][:, :part], sums[0][:, 2 * part :], sums[1][:, 2 * part : 3 * part]]
        pieces = jnp.concatenate([x.astype(bf16) for x in pieces], axis=1)
        pieces = to_ranks(pieces.reshape(ranks, weight_rows, 6 * part))
        query_grad, key_grad, value_grad, mem_key_grad, mem_value_grad, cross_grad = columns_back(
            pieces, (part,) * 6, 0
        )

        first = ((dp_own * g_size + g_own) * ranks + rank_own) * weight_rows
        vec_grads = lax.dynamic_slice_in_dim(vec_sums, first, weight_rows, axis=1)

        return (
            layer_out,
            tokens_grad,
            memory_grad,
            query_grad,
            key_grad,
            value_grad,
            own_rows_of(sums[1][:, part : 2 * part]),
            cross_grad,
            mem_key_grad,
            mem_value_grad,
            own_rows_of(sums[1][:, 3 * part :]),
            up_grad,
            down_grad,
            vec_grads[0],
            vec_grads[1],
            vec_grads[2],
            vec_grads[3],
            vec_grads[4],
            vec_grads[5],
        )

    return body


def solution(mesh):
    dp_size, seq_size = mesh.shape["dp"], mesh.shape["seq"]

    def layer_step(*args):
        g_size = args[0].shape[0] // dp_size
        z_size = seq_size // (g_size * CORES)
        split_mesh = Mesh(
            mesh.devices.reshape(dp_size, g_size, z_size, CORES), ("dp", "g", "z", "c")
        )
        seq = ("g", "z", "c")
        every = ("dp", "g", "z", "c")
        rows = P("dp", seq, None)
        matrix = P(every, None)
        vector = P(every)
        return jax.shard_map(
            make_body(dp_size, g_size, z_size),
            mesh=split_mesh,
            in_specs=(rows,) * 3 + (P("dp", None), P("dp")) + (matrix,) * 10 + (vector,) * 6,
            out_specs=(rows,) * 3 + (matrix,) * 10 + (vector,) * 6,
            check_vma=False,
        )(*args)

    return layer_step
```

profile of v0, /device:TPU:0, one launch (start us, length us, event | category | flops | bytes accessed | tf_op | source)
XLA Modules:
  0.0 380.5 jit_solution(1310969609383804434)
XLA Ops:
  8.2 4.1 %collective-permute-start = (bf16[64,1024]{1,0:T(8,128)(2,1)S(1)}, bf16[64,1024]{1,0:T(8,128)(2,1)S(1)}, u32[]{:S(2)}, u32[]{:S(2)}) collective-permute-start(bf16[64,1024]{1,0:T(8,128)(2,1)S(1)} %get-tuple-element.308), channel_id=1, source_target_pairs={{0,4},{4,0},{1,5},{5,1},{2,6},{6,2},{3,7},{7,3},{8,12},{12,8},{9,1... | collective-permute-start | bytes 393224 | tf_op jit(solution)/shard_map/ppermute | solution.py:250
  12.3 1.9 lay_out.1
  14.3 3.5 all-to-all-start
  24.5 2.0 collective-permute-start.3
  27.4 3.5 all-to-all-start.1
  30.9 7.8 %collective-permute-done.1 = bf16[128,1024]{1,0:T(8,128)(2,1)S(1)} collective-permute-done((bf16[128,1024]{1,0:T(8,128)(2,1)S(1)}, bf16[128,1024]{1,0:T(8,128)(2,1)S(1)}, u32[]{:S(2)}, u32[]{:S(2)}) %collective-permute-start.1) | collective-permute-done | bytes 262176 | tf_op jit(solution)/shard_map/ppermute | solution.py:250
  39.1 8.6 %collective-permute-done.19 = bf16[64,1024]{1,0:T(8,128)(2,1)S(1)} collective-permute-done((bf16[64,1024]{1,0:T(8,128)(2,1)S(1)}, bf16[64,1024]{1,0:T(8,128)(2,1)S(1)}, u32[]{:S(2)}, u32[]{:S(2)}) %collective-permute-start.19) | collective-permute-done | bytes 131104 | tf_op jit(solution)/shard_map/ppermute | solution.py:250
  52.6 3.1 collective-permute-done.5
  57.7 4.6 %all-to-all-start.2 = ((bf16[32,6,32]{2,1,0:T(8,128)(2,1)}), bf16[32,6,32]{2,1,0:T(8,128)(2,1)S(1)}, u32[]{:S(2)}, u32[]{:S(2)}) async-start(bf16[32,6,32]{2,1,0:T(8,128)(2,1)} %broadcast_in_dim.21), calls=%async_computation.2 | async-start | bytes 131072 | tf_op jit(solution)/shard_map/all_to_all | solution.py:575
  66.5 3.2 all-to-all-done.2
  70.0 8.3 %collective-permute-done.8 = bf16[2,2,128,512]{3,2,1,0:T(8,128)(2,1)} collective-permute-done((bf16[2,2,128,512]{3,2,1,0:T(8,128)(2,1)}, bf16[2,2,128,512]{3,2,1,0:T(8,128)(2,1)}, u32[]{:S(2)}, u32[]{:S(2)}) %collective-permute-start.8) | collective-permute-done | bytes 524320 | tf_op jit(solution)/shard_map/ppermute | solution.py:250
  79.9 2.3 collective-permute-start.12
  88.0 1.9 convolution_convert_fusion.9
  90.0 1.9 convolution_convert_fusion.10.v_ref
  91.9 5.1 %collective-permute-done.15.refs_3_ = bf16[2,4,32,256]{3,2,1,0:T(8,128)(2,1)S(1)} collective-permute-done((bf16[2,4,32,256]{3,2,1,0:T(8,128)(2,1)S(1)}, bf16[2,4,32,256]{3,2,1,0:T(8,128)(2,1)S(1)}, u32[]{:S(2)}, u32[]{:S(2)}) %collective-permute-start.15) | collective-permute-done | bytes 131104 | tf_op jit(solution)/shard_map/ppermute | solution.py:250
  97.1 2.2 attend.3
  100.4 2.2 collective-permute-start.23
  106.1 6.5 %collective-permute-done.21 = bf16[128,1024]{1,0:T(8,128)(2,1)S(1)} collective-permute-done((bf16[128,1024]{1,0:T(8,128)(2,1)S(1)}, bf16[128,1024]{1,0:T(8,128)(2,1)S(1)}, u32[]{:S(2)}, u32[]{:S(2)}) %collective-permute-start.21) | collective-permute-done | bytes 262176 | tf_op jit(solution)/shard_map/ppermute | solution.py:250
  114.7 6.2 %collective-permute-done.18.came = bf16[128,1024]{1,0:T(8,128)(2,1)S(1)} collective-permute-done((bf16[128,1024]{1,0:T(8,128)(2,1)S(1)}, bf16[128,1024]{1,0:T(8,128)(2,1)S(1)}, u32[]{:S(2)}, u32[]{:S(2)}) %collective-permute-start.18) | collective-permute-done | bytes 262176 | tf_op jit(solution)/shard_map/ppermute | solution.py:250
  122.0 6.0 %collective-permute-done.25 = bf16[2,2,128,512]{3,2,1,0:T(8,128)(2,1)S(1)} collective-permute-done((bf16[2,2,128,512]{3,2,1,0:T(8,128)(2,1)S(1)}, bf16[2,2,128,512]{3,2,1,0:T(8,128)(2,1)S(1)}, u32[]{:S(2)}, u32[]{:S(2)}) %collective-permute-start.25) | collective-permute-done | bytes 524320 | tf_op jit(solution)/shard_map/ppermute | solution.py:250
  131.3 3.5 collective-permute-done.31.refs_3_
  149.8 6.7 %collective-permute-done.36.came = bf16[128,1024]{1,0:T(8,128)(2,1)S(1)} collective-permute-done((bf16[128,1024]{1,0:T(8,128)(2,1)S(1)}, bf16[128,1024]{1,0:T(8,128)(2,1)S(1)}, u32[]{:S(2)}, u32[]{:S(2)}) %collective-permute-start.36) | collective-permute-done | bytes 262176 | tf_op jit(solution)/shard_map/ppermute | solution.py:250
  158.5 6.0 %collective-permute-done.42 = bf16[128,1024]{1,0:T(8,128)(2,1)S(1)} collective-permute-done((bf16[128,1024]{1,0:T(8,128)(2,1)S(1)}, bf16[128,1024]{1,0:T(8,128)(2,1)S(1)}, u32[]{:S(2)}, u32[]{:S(2)}) %collective-permute-start.42) | collective-permute-done | bytes 262176 | tf_op jit(solution)/shard_map/ppermute | solution.py:250
  164.5 2.3 collective-permute-done.40
  174.2 6.1 %collective-permute-done.45.came = bf16[128,1024]{1,0:T(8,128)(2,1)S(1)} collective-permute-done((bf16[128,1024]{1,0:T(8,128)(2,1)S(1)}, bf16[128,1024]{1,0:T(8,128)(2,1)S(1)}, u32[]{:S(2)}, u32[]{:S(2)}) %collective-permute-start.45) | collective-permute-done | bytes 262176 | tf_op jit(solution)/shard_map/ppermute | solution.py:250
  183.1 6.4 %collective-permute-done.48 = bf16[128,1024]{1,0:T(8,128)(2,1)S(1)} collective-permute-done((bf16[128,1024]{1,0:T(8,128)(2,1)S(1)}, bf16[128,1024]{1,0:T(8,128)(2,1)S(1)}, u32[]{:S(2)}, u32[]{:S(2)}) %collective-permute-start.48) | collective-permute-done | bytes 262176 | tf_op jit(solution)/shard_map/ppermute | solution.py:250
  196.7 2.4 pad_maximum_fusion
  199.1 3.9 %collective-permute-done.51.refs_2_ = bf16[128,1024]{1,0:T(8,128)(2,1)S(1)} collective-permute-done((bf16[128,1024]{1,0:T(8,128)(2,1)S(1)}, bf16[128,1024]{1,0:T(8,128)(2,1)S(1)}, u32[]{:S(2)}, u32[]{:S(2)}) %collective-permute-start.51) | collective-permute-done | bytes 262176 | tf_op jit(solution)/shard_map/ppermute | solution.py:250
  209.6 4.7 %collective-permute-done.54 = bf16[64,1024]{1,0:T(8,128)(2,1)} collective-permute-done((bf16[64,1024]{1,0:T(8,128)(2,1)}, bf16[64,1024]{1,0:T(8,128)(2,1)}, u32[]{:S(2)}, u32[]{:S(2)}) %collective-permute-start.54) | collective-permute-done | bytes 131104 | tf_op jit(solution)/shard_map/ppermute | solution.py:250
  224.1 2.1 attend_back.5
  230.2 6.5 %collective-permute-done.58.refs_2_ = bf16[128,1024]{1,0:T(8,128)(2,1)S(1)} collective-permute-done((bf16[128,1024]{1,0:T(8,128)(2,1)S(1)}, bf16[128,1024]{1,0:T(8,128)(2,1)S(1)}, u32[]{:S(2)}, u32[]{:S(2)}) %collective-permute-start.58) | collective-permute-done | bytes 262176 | tf_op jit(solution)/shard_map/ppermute | solution.py:250
  243.1 2.7 collective-permute-done.63
  251.7 2.1 attend_back.7
  253.7 2.0 convolution_convert_fusion.3
  262.0 2.5 collective-permute-done.67.refs_4_
  264.5 3.1 collective-permute-done.66.refs_3_
  277.2 6.2 %collective-permute-done.76 = bf16[128,1024]{1,0:T(8,128)(2,1)S(1)} collective-permute-done((bf16[128,1024]{1,0:T(8,128)(2,1)S(1)}, bf16[128,1024]{1,0:T(8,128)(2,1)S(1)}, u32[]{:S(2)}, u32[]{:S(2)}) %collective-permute-start.76) | collective-permute-done | bytes 262176 | tf_op jit(solution)/shard_map/ppermute | solution.py:250
  283.5 3.3 collective-permute-done.64
  288.6 2.4 collective-permute-start.72
  291.7 9.9 %collective-permute-done.71 = bf16[2,2,128,1024]{3,2,1,0:T(8,128)(2,1)} collective-permute-done((bf16[2,2,128,1024]{3,2,1,0:T(8,128)(2,1)}, bf16[2,2,128,1024]{3,2,1,0:T(8,128)(2,1)}, u32[]{:S(2)}, u32[]{:S(2)}) %collective-permute-start.71) | collective-permute-done | bytes 1048608 | tf_op jit(solution)/shard_map/ppermute | solution.py:250
  303.2 6.7 %collective-permute-done.72 = bf16[128,1024]{1,0:T(8,128)(2,1)S(1)} collective-permute-done((bf16[128,1024]{1,0:T(8,128)(2,1)S(1)}, bf16[128,1024]{1,0:T(8,128)(2,1)S(1)}, u32[]{:S(2)}, u32[]{:S(2)}) %collective-permute-start.72) | collective-permute-done | bytes 262176 | tf_op jit(solution)/shard_map/ppermute | solution.py:250
  310.6 3.7 collective-permute-done.73
  318.3 5.5 %collective-permute-done.77 = bf16[64,1024]{1,0:T(8,128)(2,1)S(1)} collective-permute-done((bf16[64,1024]{1,0:T(8,128)(2,1)S(1)}, bf16[64,1024]{1,0:T(8,128)(2,1)S(1)}, u32[]{:S(2)}, u32[]{:S(2)}) %collective-permute-start.77) | collective-permute-done | bytes 131104 | tf_op jit(solution)/shard_map/ppermute | solution.py:250
  327.0 3.4 all-to-all-start.4
  338.3 17.3 %collective-permute-done.83 = bf16[128,1024]{1,0:T(8,128)(2,1)S(1)} collective-permute-done((bf16[128,1024]{1,0:T(8,128)(2,1)S(1)}, bf16[128,1024]{1,0:T(8,128)(2,1)S(1)}, u32[]{:S(2)}, u32[]{:S(2)}) %collective-permute-start.83) | collective-permute-done | bytes 262176 | tf_op jit(solution)/shard_map/ppermute | solution.py:250
  355.7 5.1 %collective-permute-done.85 = bf16[128,1024]{1,0:T(8,128)(2,1)S(1)} collective-permute-done((bf16[128,1024]{1,0:T(8,128)(2,1)S(1)}, bf16[128,1024]{1,0:T(8,128)(2,1)S(1)}, u32[]{:S(2)}, u32[]{:S(2)}) %collective-permute-start.85) | collective-permute-done | bytes 262176 | tf_op jit(solution)/shard_map/ppermute | solution.py:250
  361.7 3.5 all-to-all-start.3
  368.9 3.6 all-to-all-done.3.in_ref
  (485 shorter events, 145.7 us)
Async XLA Ops:
  8.2 15.0 %collective-permute-start = (bf16[64,1024]{1,0:T(8,128)(2,1)S(1)}, bf16[64,1024]{1,0:T(8,128)(2,1)S(1)}, u32[]{:S(2)}, u32[]{:S(2)}) collective-permute-start(bf16[64,1024]{1,0:T(8,128)(2,1)S(1)} %get-tuple-element.308), channel_id=1, source_target_pairs={{0,4},{4,0},{1,5},{5,1},{2,6},{6,2},{3,7},{7,3},{8,12},{12,8},{9,1... | collective-permute-start | bytes 393224 | tf_op jit(solution)/shard_map/ppermute | solution.py:250
  23.3 15.3 %collective-permute-start.1 = (bf16[128,1024]{1,0:T(8,128)(2,1)S(1)}, bf16[128,1024]{1,0:T(8,128)(2,1)S(1)}, u32[]{:S(2)}, u32[]{:S(2)}) collective-permute-start(bf16[128,1024]{1,0:T(8,128)(2,1)S(1)} %bitcast.349), channel_id=1, source_target_pairs={{0,4},{4,0},{1,5},{5,1},{2,6},{6,2},{3,7},{7,3},{8,12},{12,8},{9,1... | collective-permute-start | bytes 786440 | tf_op jit(solution)/shard_map/ppermute | solution.py:250
  24.5 14.3 %collective-permute-start.3 = (bf16[128,1024]{1,0:T(8,128)(2,1)S(1)}, bf16[128,1024]{1,0:T(8,128)(2,1)S(1)}, u32[]{:S(2)}, u32[]{:S(2)}) collective-permute-start(bf16[128,1024]{1,0:T(8,128)(2,1)S(1)} %pad_maximum_fusion.12.res), channel_id=1, source_target_pairs={{0,2},{2,0},{1,3},{3,1},{4,6},{6,4},{5,7},{7,5},{8,10},{10,8},{9,1... | collective-permute-start | bytes 786440 | tf_op jit(solution)/shard_map/ppermute | solution.py:250
  27.4 11.7 %collective-permute-start.2 = (bf16[128,1024]{1,0:T(8,128)(2,1)S(1)}, bf16[128,1024]{1,0:T(8,128)(2,1)S(1)}, u32[]{:S(2)}, u32[]{:S(2)}) collective-permute-start(bf16[128,1024]{1,0:T(8,128)(2,1)S(1)} %pad_maximum_fusion.12.res), channel_id=1, source_target_pairs={{0,1},{1,0},{2,3},{3,2},{4,5},{5,4},{6,7},{7,6},{8,9},{9,8},{10,11... | collective-permute-start | bytes 786440 | tf_op jit(solution)/shard_map/ppermute | solution.py:250
  27.4 25.0 %all-to-all-start.1 = ((bf16[4,32,1792]{2,1,0:T(8,128)(2,1)}), bf16[4,32,1792]{2,1,0:T(8,128)(2,1)S(1)}, u32[]{:S(2)}, u32[]{:S(2)}) async-start(bf16[4,32,1792]{2,1,0:T(8,128)(2,1)} %pad_maximum_fusion.10), calls=%async_computation.1 | async-start | bytes 917504 | tf_op jit(solution)/shard_map/all_to_all | solution.py:533
  47.7 14.9 %collective-permute-start.7 = (bf16[2,128,512]{2,1,0:T(8,128)(2,1)S(1)}, bf16[2,128,512]{2,1,0:T(8,128)(2,1)S(1)}, u32[]{:S(2)}, u32[]{:S(2)}) collective-permute-start(bf16[2,128,512]{2,1,0:T(8,128)(2,1)S(1)} %get-tuple-element.139), channel_id=1, source_target_pairs={{0,16},{8,24},{16,0},{24,8},{1,17},{9,25},{17,1},{25,9},{2,18},{10... | collective-permute-start | bytes 786440 | tf_op jit(solution)/shard_map/ppermute | solution.py:250
  52.5 27.4 %collective-permute-start.9 = (bf16[128,1024]{1,0:T(8,128)(2,1)S(1)}, bf16[128,1024]{1,0:T(8,128)(2,1)}, u32[]{:S(2)}, u32[]{:S(2)}) collective-permute-start(bf16[128,1024]{1,0:T(8,128)(2,1)S(1)} %bitcast.337), channel_id=1, source_target_pairs={{0,4},{4,0},{1,5},{5,1},{2,6},{6,2},{3,7},{7,3},{8,12},{12,8},{9,1... | collective-permute-start | bytes 786440 | tf_op jit(solution)/shard_map/ppermute | solution.py:250
  56.5 13.3 %collective-permute-start.6 = (bf16[2,2,128,512]{3,2,1,0:T(8,128)(2,1)}, bf16[2,2,128,512]{3,2,1,0:T(8,128)(2,1)S(1)}, u32[]{:S(2)}, u32[]{:S(2)}) collective-permute-start(bf16[2,2,128,512]{3,2,1,0:T(8,128)(2,1)} %maximum_select_fusion.9), channel_id=1, source_target_pairs={{0,16},{8,24},{16,0},{24,8},{1,17},{9,25},{17,1},{25,9},{2,18},{10... | collective-permute-start | bytes 1572872 | tf_op jit(solution)/shard_map/ppermute | solution.py:250
  57.7 12.0 %all-to-all-start.2 = ((bf16[32,6,32]{2,1,0:T(8,128)(2,1)}), bf16[32,6,32]{2,1,0:T(8,128)(2,1)S(1)}, u32[]{:S(2)}, u32[]{:S(2)}) async-start(bf16[32,6,32]{2,1,0:T(8,128)(2,1)} %broadcast_in_dim.21), calls=%async_computation.2 | async-start | bytes 131072 | tf_op jit(solution)/shard_map/all_to_all | solution.py:575
  62.3 224.9 %reduce-scatter.2.cloned.1.call-start = ((), (), s32[]{:S(2)}) async-start(), calls=%async_computation.6 | async-start | bytes 5242880 | tf_op jit(solution)/shard_map/reduce_scatter | solution.py:689
  63.5 14.8 %collective-permute-start.8 = (bf16[2,2,128,512]{3,2,1,0:T(8,128)(2,1)}, bf16[2,2,128,512]{3,2,1,0:T(8,128)(2,1)}, u32[]{:S(2)}, u32[]{:S(2)}) collective-permute-start(bf16[2,2,128,512]{3,2,1,0:T(8,128)(2,1)} %maximum_select_fusion.11), channel_id=1, source_target_pairs={{0,8},{8,0},{16,24},{24,16},{1,9},{9,1},{17,25},{25,17},{2,10},{10... | collective-permute-start | bytes 1572872 | tf_op jit(solution)/shard_map/ppermute | solution.py:250
  79.9 20.5 %collective-permute-start.12 = (bf16[128,1024]{1,0:T(8,128)(2,1)S(1)}, bf16[128,1024]{1,0:T(8,128)(2,1)S(1)}, u32[]{:S(2)}, u32[]{:S(2)}) collective-permute-start(bf16[128,1024]{1,0:T(8,128)(2,1)S(1)} %bitcast.321), channel_id=1, source_target_pairs={{0,4},{4,0},{1,5},{5,1},{2,6},{6,2},{3,7},{7,3},{8,12},{12,8},{9,1... | collective-permute-start | bytes 786440 | tf_op jit(solution)/shard_map/ppermute | solution.py:250
  83.3 19.3 %collective-permute-start.11 = (bf16[2,128,512]{2,1,0:T(8,128)(2,1)S(1)}, bf16[2,128,512]{2,1,0:T(8,128)(2,1)S(1)}, u32[]{:S(2)}, u32[]{:S(2)}) collective-permute-start(bf16[2,128,512]{2,1,0:T(8,128)(2,1)S(1)} %get-tuple-element.275), channel_id=1, source_target_pairs={{0,16},{8,24},{16,0},{24,8},{1,17},{9,25},{17,1},{25,9},{2,18},{10... | collective-permute-start | bytes 786440 | tf_op jit(solution)/shard_map/ppermute | solution.py:250
  84.9 17.8 %collective-permute-start.10 = (bf16[2,128,512]{2,1,0:T(8,128)(2,1)S(1)}, bf16[2,128,512]{2,1,0:T(8,128)(2,1)S(1)}, u32[]{:S(2)}, u32[]{:S(2)}) collective-permute-start(bf16[2,128,512]{2,1,0:T(8,128)(2,1)S(1)} %get-tuple-element.278), channel_id=1, source_target_pairs={{0,8},{8,0},{16,24},{24,16},{1,9},{9,1},{17,25},{25,17},{2,10},{10... | collective-permute-start | bytes 786440 | tf_op jit(solution)/shard_map/ppermute | solution.py:250
  86.3 10.6 %collective-permute-start.15 = (bf16[2,4,32,256]{3,2,1,0:T(8,128)(2,1)S(1)}, bf16[2,4,32,256]{3,2,1,0:T(8,128)(2,1)S(1)}, u32[]{:S(2)}, u32[]{:S(2)}) collective-permute-start(bf16[2,4,32,256]{3,2,1,0:T(8,128)(2,1)S(1)} %get-tuple-element.281), channel_id=1, source_target_pairs={{0,3},{1,2},{2,1},{3,0},{4,7},{5,6},{6,5},{7,4},{8,11},{9,10},{10,... | collective-permute-start | bytes 393224 | tf_op jit(solution)/shard_map/ppermute | solution.py:250
  86.4 13.4 %collective-permute-start.14 = (bf16[2,4,32,256]{3,2,1,0:T(8,128)(2,1)S(1)}, bf16[2,4,32,256]{3,2,1,0:T(8,128)(2,1)S(1)}, u32[]{:S(2)}, u32[]{:S(2)}) collective-permute-start(bf16[2,4,32,256]{3,2,1,0:T(8,128)(2,1)S(1)} %get-tuple-element.282), channel_id=1, source_target_pairs={{0,2},{1,3},{2,0},{3,1},{4,6},{5,7},{6,4},{7,5},{8,10},{9,11},{10,... | collective-permute-start | bytes 393224 | tf_op jit(solution)/shard_map/ppermute | solution.py:250
  99.8 12.7 %collective-permute-start.21 = (bf16[128,1024]{1,0:T(8,128)(2,1)S(1)}, bf16[128,1024]{1,0:T(8,128)(2,1)S(1)}, u32[]{:S(2)}, u32[]{:S(2)}) collective-permute-start(bf16[128,1024]{1,0:T(8,128)(2,1)S(1)} %pad_maximum_fusion.14), channel_id=1, source_target_pairs={{0,2},{2,0},{1,3},{3,1},{4,6},{6,4},{5,7},{7,5},{8,10},{10,8},{9,1... | collective-permute-start | bytes 786440 | tf_op jit(solution)/shard_map/ppermute | solution.py:250
  100.4 20.5 %collective-permute-start.23 = (bf16[128,1024]{1,0:T(8,128)(2,1)S(1)}, bf16[128,1024]{1,0:T(8,128)(2,1)S(1)}, u32[]{:S(2)}, u32[]{:S(2)}) collective-permute-start(bf16[128,1024]{1,0:T(8,128)(2,1)S(1)} %copy-done.45), channel_id=1, source_target_pairs={{0,4},{4,0},{1,5},{5,1},{2,6},{6,2},{3,7},{7,3},{8,12},{12,8},{9,1... | collective-permute-start | bytes 786440 | tf_op jit(solution)/shard_map/ppermute | solution.py:250
  102.9 27.5 %collective-permute-start.32 = (bf16[2,128,1024]{2,1,0:T(8,128)(2,1)S(1)}, bf16[2,128,1024]{2,1,0:T(8,128)(2,1)S(1)}, u32[]{:S(2)}, u32[]{:S(2)}) collective-permute-start(bf16[2,128,1024]{2,1,0:T(8,128)(2,1)S(1)} %maximum_select_fusion.16), channel_id=1, source_target_pairs={{0,8},{8,0},{16,24},{24,16},{1,9},{9,1},{17,25},{25,17},{2,10},{10... | collective-permute-start | bytes 1572872 | tf_op jit(solution)/shard_map/ppermute | solution.py:250
  112.7 15.3 %collective-permute-start.25 = (bf16[2,2,128,512]{3,2,1,0:T(8,128)(2,1)S(1)}, bf16[2,2,128,512]{3,2,1,0:T(8,128)(2,1)S(1)}, u32[]{:S(2)}, u32[]{:S(2)}) collective-permute-start(bf16[2,2,128,512]{3,2,1,0:T(8,128)(2,1)S(1)} %maximum_select_fusion.15), channel_id=1, source_target_pairs={{0,8},{8,0},{16,24},{24,16},{1,9},{9,1},{17,25},{25,17},{2,10},{10... | collective-permute-start | bytes 1572872 | tf_op jit(solution)/shard_map/ppermute | solution.py:250
  114.1 14.8 %collective-permute-start.28 = (bf16[2,2,128,512]{3,2,1,0:T(8,128)(2,1)S(1)}, bf16[2,2,128,512]{3,2,1,0:T(8,128)(2,1)S(1)}, u32[]{:S(2)}, u32[]{:S(2)}) collective-permute-start(bf16[2,2,128,512]{3,2,1,0:T(8,128)(2,1)S(1)} %maximum_select_fusion.14), channel_id=1, source_target_pairs={{0,16},{8,24},{16,0},{24,8},{1,17},{9,25},{17,1},{25,9},{2,18},{10... | collective-permute-start | bytes 1572872 | tf_op jit(solution)/shard_map/ppermute | solution.py:250
  121.2 13.6 %collective-permute-start.26 = (bf16[128,1024]{1,0:T(8,128)(2,1)S(1)}, bf16[128,1024]{1,0:T(8,128)(2,1)S(1)}, u32[]{:S(2)}, u32[]{:S(2)}) collective-permute-start(bf16[128,1024]{1,0:T(8,128)(2,1)S(1)} %get-tuple-element.159.res), channel_id=1, source_target_pairs={{0,2},{2,0},{1,3},{3,1},{4,6},{6,4},{5,7},{7,5},{8,10},{10,8},{9,1... | collective-permute-start | bytes 786440 | tf_op jit(solution)/shard_map/ppermute | solution.py:250
  121.3 17.8 %collective-permute-start.24 = (bf16[128,1024]{1,0:T(8,128)(2,1)S(1)}, bf16[128,1024]{1,0:T(8,128)(2,1)S(1)}, u32[]{:S(2)}, u32[]{:S(2)}) collective-permute-start(bf16[128,1024]{1,0:T(8,128)(2,1)S(1)} %get-tuple-element.159.res), channel_id=1, source_target_pairs={{0,1},{1,0},{2,3},{3,2},{4,5},{5,4},{6,7},{7,6},{8,9},{9,8},{10,11... | collective-permute-start | bytes 786440 | tf_op jit(solution)/shard_map/ppermute | solution.py:250
  128.0 13.1 %collective-permute-start.33 = (bf16[2,128,1024]{2,1,0:T(8,128)(2,1)S(1)}, bf16[2,128,1024]{2,1,0:T(8,128)(2,1)S(1)}, u32[]{:S(2)}, u32[]{:S(2)}) collective-permute-start(bf16[2,128,1024]{2,1,0:T(8,128)(2,1)S(1)} %maximum_select_fusion.18), channel_id=1, source_target_pairs={{0,16},{8,24},{16,0},{24,8},{1,17},{9,25},{17,1},{25,9},{2,18},{10... | collective-permute-start | bytes 1572872 | tf_op jit(solution)/shard_map/ppermute | solution.py:250
  137.0 12.7 %collective-permute-start.37 = (bf16[64,1024]{1,0:T(8,128)(2,1)S(1)}, bf16[64,1024]{1,0:T(8,128)(2,1)S(1)}, u32[]{:S(2)}, u32[]{:S(2)}) collective-permute-start(bf16[64,1024]{1,0:T(8,128)(2,1)S(1)} %get-tuple-element.304), channel_id=1, source_target_pairs={{0,4},{4,0},{1,5},{5,1},{2,6},{6,2},{3,7},{7,3},{8,12},{12,8},{9,1... | collective-permute-start | bytes 393224 | tf_op jit(solution)/shard_map/ppermute | solution.py:250
  141.6 25.9 %collective-permute-start.39 = (bf16[2,2,128,1024]{3,2,1,0:T(8,128)(2,1)S(1)}, bf16[2,2,128,1024]{3,2,1,0:T(8,128)(2,1)S(1)}, u32[]{:S(2)}, u32[]{:S(2)}) collective-permute-start(bf16[2,2,128,1024]{3,2,1,0:T(8,128)(2,1)S(1)} %maximum_select_fusion.6), channel_id=1, source_target_pairs={{0,16},{8,24},{16,0},{24,8},{1,17},{9,25},{17,1},{25,9},{2,18},{10... | collective-permute-start | bytes 3145736 | tf_op jit(solution)/shard_map/ppermute | solution.py:250
  142.2 24.6 %collective-permute-start.40 = (bf16[2,2,128,1024]{3,2,1,0:T(8,128)(2,1)S(1)}, bf16[2,2,128,1024]{3,2,1,0:T(8,128)(2,1)S(1)}, u32[]{:S(2)}, u32[]{:S(2)}) collective-permute-start(bf16[2,2,128,1024]{3,2,1,0:T(8,128)(2,1)S(1)} %maximum_select_fusion.7), channel_id=1, source_target_pairs={{0,8},{8,0},{16,24},{24,16},{1,9},{9,1},{17,25},{25,17},{2,10},{10... | collective-permute-start | bytes 3145736 | tf_op jit(solution)/shard_map/ppermute | solution.py:250
  158.5 11.1 %collective-permute-start.38 = (bf16[128,1024]{1,0:T(8,128)(2,1)S(1)}, bf16[128,1024]{1,0:T(8,128)(2,1)S(1)}, u32[]{:S(2)}, u32[]{:S(2)}) collective-permute-start(bf16[128,1024]{1,0:T(8,128)(2,1)S(1)} %get-tuple-element.174.res), channel_id=1, source_target_pairs={{0,1},{1,0},{2,3},{3,2},{4,5},{5,4},{6,7},{7,6},{8,9},{9,8},{10,11... | collective-permute-start | bytes 786440 | tf_op jit(solution)/shard_map/ppermute | solution.py:250
  206.8 14.1 %collective-permute-start.52 = (bf16[128,1024]{1,0:T(8,128)(2,1)}, bf16[128,1024]{1,0:T(8,128)(2,1)}, u32[]{:S(2)}, u32[]{:S(2)}) collective-permute-start(bf16[128,1024]{1,0:T(8,128)(2,1)} %copy-done.19), channel_id=1, source_target_pairs={{0,2},{2,0},{1,3},{3,1},{4,6},{6,4},{5,7},{7,5},{8,10},{10,8},{9,1... | collective-permute-start | bytes 786440 | tf_op jit(solution)/shard_map/ppermute | solution.py:250
  237.5 10.7 %collective-permute-start.60 = (bf16[128,1024]{1,0:T(8,128)(2,1)S(1)}, bf16[128,1024]{1,0:T(8,128)(2,1)S(1)}, u32[]{:S(2)}, u32[]{:S(2)}) collective-permute-start(bf16[128,1024]{1,0:T(8,128)(2,1)S(1)} %get-tuple-element.211), channel_id=1, source_target_pairs={{0,2},{2,0},{1,3},{3,1},{4,6},{6,4},{5,7},{7,5},{8,10},{10,8},{9,1... | collective-permute-start | bytes 786440 | tf_op jit(solution)/shard_map/ppermute | solution.py:250
  237.8 10.4 %collective-permute-start.59 = (bf16[128,1024]{1,0:T(8,128)(2,1)S(1)}, bf16[128,1024]{1,0:T(8,128)(2,1)S(1)}, u32[]{:S(2)}, u32[]{:S(2)}) collective-permute-start(bf16[128,1024]{1,0:T(8,128)(2,1)S(1)} %get-tuple-element.211), channel_id=1, source_target_pairs={{0,1},{1,0},{2,3},{3,2},{4,5},{5,4},{6,7},{7,6},{8,9},{9,8},{10,11... | collective-permute-start | bytes 786440 | tf_op jit(solution)/shard_map/ppermute | solution.py:250
  240.4 10.3 %collective-permute-start.79 = (bf16[128,1024]{1,0:T(8,128)(2,1)S(1)}, bf16[128,1024]{1,0:T(8,128)(2,1)S(1)}, u32[]{:S(2)}, u32[]{:S(2)}) collective-permute-start(bf16[128,1024]{1,0:T(8,128)(2,1)S(1)} %slice.442), channel_id=1, source_target_pairs={{0,1},{1,0},{2,3},{3,2},{4,5},{5,4},{6,7},{7,6},{8,9},{9,8},{10,11... | collective-permute-start | bytes 786440 | tf_op jit(solution)/shard_map/ppermute | solution.py:250
  242.3 18.6 %collective-permute-start.70 = (bf16[2,32,1024]{2,1,0:T(8,128)(2,1)S(1)}, bf16[2,32,1024]{2,1,0:T(8,128)(2,1)S(1)}, u32[]{:S(2)}, u32[]{:S(2)}) collective-permute-start(bf16[2,32,1024]{2,1,0:T(8,128)(2,1)S(1)} %get-tuple-element.259), channel_id=1, source_target_pairs={{0,3},{1,2},{2,1},{3,0},{4,7},{5,6},{6,5},{7,4},{8,11},{9,10},{10,... | collective-permute-start | bytes 393224 | tf_op jit(solution)/shard_map/ppermute | solution.py:250
  245.8 15.4 %collective-permute-start.69 = (bf16[2,32,1024]{2,1,0:T(8,128)(2,1)S(1)}, bf16[2,32,1024]{2,1,0:T(8,128)(2,1)S(1)}, u32[]{:S(2)}, u32[]{:S(2)}) collective-permute-start(bf16[2,32,1024]{2,1,0:T(8,128)(2,1)S(1)} %get-tuple-element.260), channel_id=1, source_target_pairs={{0,2},{1,3},{2,0},{3,1},{4,6},{5,7},{6,4},{7,5},{8,10},{9,11},{10,... | collective-permute-start | bytes 393224 | tf_op jit(solution)/shard_map/ppermute | solution.py:250
  248.2 13.9 %collective-permute-start.68 = (bf16[2,32,1024]{2,1,0:T(8,128)(2,1)S(1)}, bf16[2,32,1024]{2,1,0:T(8,128)(2,1)S(1)}, u32[]{:S(2)}, u32[]{:S(2)}) collective-permute-start(bf16[2,32,1024]{2,1,0:T(8,128)(2,1)S(1)} %get-tuple-element.261), channel_id=1, source_target_pairs={{0,1},{1,0},{2,3},{3,2},{4,5},{5,4},{6,7},{7,6},{8,9},{9,8},{10,11... | collective-permute-start | bytes 393224 | tf_op jit(solution)/shard_map/ppermute | solution.py:250
  261.2 25.6 %collective-permute-start.64 = (bf16[2,2,128,1024]{3,2,1,0:T(8,128)(2,1)S(1)}, bf16[2,2,128,1024]{3,2,1,0:T(8,128)(2,1)S(1)}, u32[]{:S(2)}, u32[]{:S(2)}) collective-permute-start(bf16[2,2,128,1024]{3,2,1,0:T(8,128)(2,1)S(1)} %dynamic-slice_bitcast_fusion.1), channel_id=1, source_target_pairs={{0,8},{8,0},{16,24},{24,16},{1,9},{9,1},{17,25},{25,17},{2,10},{10... | collective-permute-start | bytes 3145736 | tf_op jit(solution)/shard_map/ppermute | solution.py:250
  272.2 11.2 %collective-permute-start.76 = (bf16[128,1024]{1,0:T(8,128)(2,1)S(1)}, bf16[128,1024]{1,0:T(8,128)(2,1)S(1)}, u32[]{:S(2)}, u32[]{:S(2)}) collective-permute-start(bf16[128,1024]{1,0:T(8,128)(2,1)S(1)} %fusion.52), channel_id=1, source_target_pairs={{0,2},{2,0},{1,3},{3,1},{4,6},{6,4},{5,7},{7,5},{8,10},{10,8},{9,1... | collective-permute-start | bytes 786440 | tf_op jit(solution)/shard_map/ppermute | solution.py:250
  274.6 43.7 %collective-permute-start.81 = (bf16[64,1024]{1,0:T(8,128)(2,1)}, bf16[64,1024]{1,0:T(8,128)(2,1)}, u32[]{:S(2)}, u32[]{:S(2)}) collective-permute-start(bf16[64,1024]{1,0:T(8,128)(2,1)} %get-tuple-element.293), channel_id=1, source_target_pairs={{0,4},{4,0},{1,5},{5,1},{2,6},{6,2},{3,7},{7,3},{8,12},{12,8},{9,1... | collective-permute-start | bytes 393224 | tf_op jit(solution)/shard_map/ppermute | solution.py:250
  276.6 25.0 %collective-permute-start.71 = (bf16[2,2,128,1024]{3,2,1,0:T(8,128)(2,1)}, bf16[2,2,128,1024]{3,2,1,0:T(8,128)(2,1)}, u32[]{:S(2)}, u32[]{:S(2)}) collective-permute-start(bf16[2,2,128,1024]{3,2,1,0:T(8,128)(2,1)} %dynamic-slice_bitcast_fusion), channel_id=1, source_target_pairs={{0,16},{8,24},{16,0},{24,8},{1,17},{9,25},{17,1},{25,9},{2,18},{10... | collective-permute-start | bytes 3145736 | tf_op jit(solution)/shard_map/ppermute | solution.py:250
  288.6 21.3 %collective-permute-start.72 = (bf16[128,1024]{1,0:T(8,128)(2,1)S(1)}, bf16[128,1024]{1,0:T(8,128)(2,1)S(1)}, u32[]{:S(2)}, u32[]{:S(2)}) collective-permute-start(bf16[128,1024]{1,0:T(8,128)(2,1)S(1)} %dynamic-slice_bitcast_fusion.7), channel_id=1, source_target_pairs={{0,4},{4,0},{1,5},{5,1},{2,6},{6,2},{3,7},{7,3},{8,12},{12,8},{9,1... | collective-permute-start | bytes 786440 | tf_op jit(solution)/shard_map/ppermute | solution.py:250
  291.0 23.4 %collective-permute-start.73 = (bf16[128,1024]{1,0:T(8,128)(2,1)S(1)}, bf16[128,1024]{1,0:T(8,128)(2,1)S(1)}, u32[]{:S(2)}, u32[]{:S(2)}) collective-permute-start(bf16[128,1024]{1,0:T(8,128)(2,1)S(1)} %dynamic-slice_bitcast_fusion.6), channel_id=1, source_target_pairs={{0,4},{4,0},{1,5},{5,1},{2,6},{6,2},{3,7},{7,3},{8,12},{12,8},{9,1... | collective-permute-start | bytes 786440 | tf_op jit(solution)/shard_map/ppermute | solution.py:250
  316.1 16.6 %collective-permute-start.82 = (bf16[2,128,1024]{2,1,0:T(8,128)(2,1)}, bf16[2,128,1024]{2,1,0:T(8,128)(2,1)}, u32[]{:S(2)}, u32[]{:S(2)}) collective-permute-start(bf16[2,128,1024]{2,1,0:T(8,128)(2,1)} %dynamic-slice_bitcast_fusion.3), channel_id=1, source_target_pairs={{0,16},{8,24},{16,0},{24,8},{1,17},{9,25},{17,1},{25,9},{2,18},{10... | collective-permute-start | bytes 1572872 | tf_op jit(solution)/shard_map/ppermute | solution.py:250
  317.4 17.8 %collective-permute-start.84 = (bf16[2,128,1024]{2,1,0:T(8,128)(2,1)}, bf16[2,128,1024]{2,1,0:T(8,128)(2,1)}, u32[]{:S(2)}, u32[]{:S(2)}) collective-permute-start(bf16[2,128,1024]{2,1,0:T(8,128)(2,1)} %dynamic-slice_bitcast_fusion.2), channel_id=1, source_target_pairs={{0,8},{8,0},{16,24},{24,16},{1,9},{9,1},{17,25},{25,17},{2,10},{10... | collective-permute-start | bytes 1572872 | tf_op jit(solution)/shard_map/ppermute | solution.py:250
  327.0 34.6 %all-to-all-start.4 = ((bf16[4,32,1024]{2,1,0:T(8,128)(2,1)}), bf16[4,32,1024]{2,1,0:T(8,128)(2,1)S(1)}, u32[]{:S(2)}, u32[]{:S(2)}) async-start(bf16[4,32,1024]{2,1,0:T(8,128)(2,1)} %bitcast.131), calls=%async_computation.5 | async-start | bytes 524288 | tf_op jit(solution)/shard_map/all_to_all | solution.py:533
  330.9 34.9 %collective-permute-start.88 = (f32[6,1024]{1,0:T(8,128)S(1)}, f32[6,1024]{1,0:T(8,128)S(1)}, u32[]{:S(2)}, u32[]{:S(2)}) collective-permute-start(f32[6,1024]{1,0:T(8,128)S(1)} %add.303), channel_id=1, source_target_pairs={{0,4},{4,0},{1,5},{5,1},{2,6},{6,2},{3,7},{7,3},{8,12},{12,8},{9,1... | collective-permute-start | bytes 73736 | tf_op jit(solution)/shard_map/ppermute | solution.py:250
  333.9 21.7 %collective-permute-start.83 = (bf16[128,1024]{1,0:T(8,128)(2,1)S(1)}, bf16[128,1024]{1,0:T(8,128)(2,1)S(1)}, u32[]{:S(2)}, u32[]{:S(2)}) collective-permute-start(bf16[128,1024]{1,0:T(8,128)(2,1)S(1)} %dynamic-slice_bitcast_fusion.5), channel_id=1, source_target_pairs={{0,4},{4,0},{1,5},{5,1},{2,6},{6,2},{3,7},{7,3},{8,12},{12,8},{9,1... | collective-permute-start | bytes 786440 | tf_op jit(solution)/shard_map/ppermute | solution.py:250
  336.5 24.3 %collective-permute-start.85 = (bf16[128,1024]{1,0:T(8,128)(2,1)S(1)}, bf16[128,1024]{1,0:T(8,128)(2,1)S(1)}, u32[]{:S(2)}, u32[]{:S(2)}) collective-permute-start(bf16[128,1024]{1,0:T(8,128)(2,1)S(1)} %dynamic-slice_bitcast_fusion.4), channel_id=1, source_target_pairs={{0,4},{4,0},{1,5},{5,1},{2,6},{6,2},{3,7},{7,3},{8,12},{12,8},{9,1... | collective-permute-start | bytes 786440 | tf_op jit(solution)/shard_map/ppermute | solution.py:250
  361.7 10.9 %all-to-all-start.3 = ((bf16[4,32,1536]{2,1,0:T(8,128)(2,1)}), bf16[4,32,1536]{2,1,0:T(8,128)(2,1)S(1)}, u32[]{:S(2)}, u32[]{:S(2)}) async-start(bf16[4,32,1536]{2,1,0:T(8,128)(2,1)} %bitcast.126), calls=%async_computation.4 | async-start | bytes 786432 | tf_op jit(solution)/shard_map/all_to_all | solution.py:533
  (107 other events, 726.1 us)
Sparse Core Ops, SparseCore 0:
  209.7 50.3 reduce-scatter.1
where the time goes:
time: 385 us; the launch traced here: 381 us
  waiting for transfers between devices  181 us (47%)
  starting transfers between devices  81 us (21%)
  other arithmetic  29 us (8%)
  matrix products  26.6 us (7%)
  local copies, waits for them, and re-layouts  24.5 us (6%)
  Pallas kernels  22 us (6%)
  between operations  16.6 us (4%)
    ppermute x89, waiting for transfers between devices, swap(): return lax.ppermute(values, name, [(i, i ^ flip) for i in range(size)])  174 us
    ppermute x89, starting transfers between devices, swap(): return lax.ppermute(values, name, [(i, i ^ flip) for i in range(size)])  62.1 us
    all_to_all x4, starting transfers between devices, to_ranks(): return lax.all_to_all(parts_in, ('z', 'c'), 0, 0, tiled=True)  13.9 us
    pallas_call x10, Pallas kernels, chip_call(): pl.pallas_call(kernel, in_specs=[SCALAR] * len(scalars) + [WHOLE] * len(a...  13.7 us
    dot_general x13, matrix products, matmul(): return jnp.dot(first_mat, second_mat, preferred_element_type=f32)  9.58 us
    dot_general x16, matrix products, transposed_product(): lax.dot_general(first_mat, second_mat, (((1,), (1,)), ((), ())), preferre...  8.56 us
    dot_general x8, matrix products, outer_product_sum(): lax.dot_general(first_mat, second_mat, (((0,), (0,)), ((), ())), preferre...  8.49 us
    unnamed x128, local copies, waits for them, and re-layouts  8.14 us
  transfers between devices with their start and end apart: 95, of which 42 were waited for; matrix products, arithmetic and copies ran while one was open for 19% of the time, Pallas kernels for 5%

commit v1 on v0

--- a/solution.py
+++ b/solution.py
@@ -144,7 +144,7 @@
     return chip_call(kernel, outs, "norm_turn", residual, kept, came, vectors, cotangent)
 
 
-def norm_back(grad_prev, kept, came, normed, inv_std, vectors, row):
+def norm_back(grad_prev, kept, came, normed, inv_std, vectors, row, limit=LIMIT):
     shape = grad_prev.shape
     args = [grad_prev, kept, came, normed, inv_std]
 
@@ -169,7 +169,7 @@
         out_specs=[WHOLE] * 3,
         out_shape=[pltpu.VMEM(x, dtype) for x, dtype in outs],
         scratch_shapes=[pltpu.VMEM(x.shape, x.dtype) for x in args] + [pltpu.SemaphoreType.DMA((5,))],
-        compiler_params=LIMIT,
+        compiler_params=limit,
         name="norm_back",
     )(*args, on_chip(vectors))
 
@@ -361,6 +361,17 @@
                         places.append((len(args) + r, (p, slice(None), slice(b * part, (b + 1) * part)), (r, sets, p), at))
             args += one
             first += part
+        elif one.ndim == 4:
+            ranks, sets, rows, width = one.shape
+            part = width // ranks
+            for r in range(ranks):
+                for p in range(sets):
+                    for b in range(ranks):
+                        at = slice(b * rows, (b + 1) * rows), slice(first, first + part)
+                        source = (r, p, slice(None), slice(b * part, (b + 1) * part))
+                        places.append((len(args), source, r * sets + p, at))
+            args.append(one)
+            first += part
         else:
             groups, n, m = one.shape
             places.append((len(args), (slice(None),) * 3, None, (slice(None), slice(first, first + m))))
@@ -370,7 +381,9 @@
     def copies(own, refs, out):
         found = []
         for i, source, piece, at in places:
-            lead = slice(None) if piece is None else (own ^ piece[0]) * piece[1] + piece[2]
+            lead = slice(None) if piece is None else piece
+            if isinstance(piece, tuple):
+                lead = (own ^ piece[0]) * piece[1] + piece[2]
             found.append((refs[i].at[source], out.at[(lead,) + at]))
         return found
 
@@ -500,11 +513,11 @@
             kept, last, filled = lax.optimization_barrier((sums[0], came[0], filled))
             return kept, last, filled
 
-        def bring_home(values):
+        def bring_home(values, *after):
             got = []
             for f in range(g_size):
                 piece = lax.dynamic_index_in_dim(values, g_own ^ f, 0, keepdims=False)
-                got.append(piece if f == 0 else swap(piece, "g", g_size, f))
+                got.append(piece if f == 0 else tie(swap(piece, "g", g_size, f), *after))
             return jnp.concatenate(got, axis=-2)
 
         def send_back(values):
@@ -568,15 +581,17 @@
         cross_set = jnp.concatenate([other_own[..., : 3 * part], co_parts], axis=2)
         cross_set = cross_set.reshape(rank_rows, 4 * part)
         cross_other = swap_groups(cross_set)
+        own_memory = bring_home(tie(memory, self_set), *self_pair)
+        all_tokens = jnp.concatenate(token_blocks, axis=0)
         vectors = jnp.stack(
             [attn_gain, attn_bias, cross_gain, cross_bias, feedforward_norm_gain, ffn_bias]
         )
         vectors = jnp.broadcast_to(vectors[None], (groups * ranks,) + vectors.shape)
-        vectors = lax.all_to_all(tie(vectors, self_pair[0]), every, 0, 0, tiled=True)
+        self_pair[0], self_pair[1], vectors = sync(*self_pair, vectors)
+        vectors = lax.all_to_all(vectors, every, 0, 0, tiled=True)
         vectors = vectors.transpose(1, 0, 2).reshape(6, width).astype(f32)
-        own_memory = bring_home(tie(memory, self_set))
-        all_tokens = jnp.concatenate(token_blocks, axis=0)
         self_pair = last_stage(self_pair)
+        self_pair[0], self_pair[1], vectors = sync(*self_pair, vectors)
         cross_other = tie(cross_other, *self_pair)
         w_qk = self_pair[0].reshape(width, 2 * part)
         w_v = self_pair[1][..., :part].reshape(width, part)
@@ -689,11 +704,12 @@
         ffn_grads = lax.psum_scatter(
             ffn_grads.reshape(groups * 2 * rank_rows, ff_part), "dp", scatter_dimension=0, tiled=True
         )
-        grad_two, branch, sums_two = norm_back(grad_three, kept, came, normed_two, inv_two, vectors, 2)
+        grad_two, branch, sums_two = norm_back(
+            grad_three, kept, came, normed_two, inv_two, vectors, 2, ALL_OF_IT
+        )
         layer_out = send_back(tie(layer_rows, branch))
 
         branch_blocks = gather_rows(branch)
-        branch_blocks[-1], layer_out = sync(branch_blocks[-1], layer_out)
         grad_crossed = [transposed_product(x, w_cout).astype(bf16) for x in branch_blocks]
         grad_cross_rows, sums = [], []
         for b in range(z_size):
@@ -710,6 +726,7 @@
         kept, came, cout_grad = sum_rows(
             grad_cross_rows, lambda x: transposed_product(x, w_cq), cout_gradient
         )
+        kept, layer_out = sync(kept, layer_out)
         grad_one, branch, sums_one = norm_back(grad_two, kept, came, normed_one, inv_one, vectors, 0)
         branch_blocks = gather_rows(branch)
         cout_grad = tie(cout_grad, branch).reshape(sets, ranks, weight_rows, width)
@@ -768,25 +785,24 @@
         grads_a = pack_grads(rank_own, by_group(qk_grad), by_group(mem_kv_grad))
         v_grad = outer_product_sum(all_tokens, grad_values).astype(bf16)
         grads_b = pack_grads(rank_own, by_group(v_grad), sout_pieces, by_group(cross_grad), cout_pieces)
+        grads_a, grads_b, ffn_grads = sync(grads_a, grads_b, ffn_grads)
         sums = first_sums([grads_a, grads_b])
-
-        sent = (grads_a, grads_b)
-        ffn_grads = tie(ffn_grads, *sent).reshape(g_size, 2, rank_rows, ff_part)
-        up_grad = scatter_axes(ffn_grads[:, 0], g_axes, g_axes)
-        down_grad = scatter_axes(ffn_grads[:, 1], g_axes, g_axes)
-        row_pairs = zip(row_blocks(tie(grad_qk, *sent)), row_blocks(grad_values))
+        ffn_grads = ffn_grads.reshape(g_size, 2, rank_rows, ff_part)
+        ffn_grads = scatter_axes(ffn_grads, g_axes, g_axes)
+        up_grad, down_grad = ffn_grads[0], ffn_grads[1]
+
+        row_pairs = zip(row_blocks(tie(grad_qk, grads_a, grads_b)), row_blocks(grad_values))
         kept, came = sum_rows(
             list(row_pairs),
             lambda x: transposed_product(x[0], w_qk) + transposed_product(x[1], w_v),
         )
         tokens_grad = (residual_scale * grad_one + (kept + came.astype(f32))).astype(bf16)
-        memory_grad = send_back(tie(memory_rows, *sent))
-        sums[0], sums[1], up_grad, down_grad, tokens_grad = sync(*sums, up_grad, down_grad, tokens_grad)
-
+        sums[0], sums[1], tokens_grad, memory_rows = sync(*sums, tokens_grad, memory_rows)
         sums = more_sums(sums)
-        up_pieces = to_ranks(up_grad.astype(bf16).reshape(ranks, weight_rows, ff_part))
         tokens_grad = send_back(tokens_grad)
-        vec_sums = tie(vec_sums, tokens_grad)
+        memory_grad = send_back(memory_rows)
+        up_pieces = to_ranks(tie(up_grad, *sums).astype(bf16).reshape(ranks, weight_rows, ff_part))
+        vec_sums = tie(vec_sums, *sums)
         for name, size in (("c", CORES), ("z", z_size), ("g", g_size)):
             for flip in flip_bits(size):
                 vec_sums = vec_sums + swap(vec_sums, name, size, flip)

time: 385 us -> 355 us (0.922)
  waiting for transfers between devices: 181 us -> 157 us
  other arithmetic: 29 us -> 20.5 us
    ppermute x89 -> x88, waiting for transfers between devices: 174 us -> 145 us  [swap(): return lax.ppermute(values, name, [(i, i ^ flip) for i in range(size)])]
    all_to_all x1, waiting for transfers between devices: 3.19 us -> 8.37 us  [body(): vectors = lax.all_to_all(vectors, every, 0, 0, tiled=True)]
    ppermute x89 -> x88, starting transfers between devices: 62.1 us -> 66.9 us  [swap(): return lax.ppermute(values, name, [(i, i ^ flip) for i in range(size)])]
    unnamed x128 -> x141, local copies, waits for them, and re-layouts: 8.14 us -> 10.4 us
  transfers between devices with their start and end apart: 95 -> 94, of which waited for: 42 -> 43; matrix products, arithmetic and copies ran while one was open for 19% -> 17% of each run, Pallas kernels for 5% -> 6%
where the time goes in v1:
time: 355 us; the launch traced here: 352 us
  waiting for transfers between devices  157 us (44%)
  starting transfers between devices  84.2 us (24%)
  matrix products  26.8 us (8%)
  local copies, waits for them, and re-layouts  23.8 us (7%)
  Pallas kernels  23.3 us (7%)
  other arithmetic  20.5 us (6%)
  between operations  16.6 us (5%)
    ppermute x88, waiting for transfers between devices, swap(): return lax.ppermute(values, name, [(i, i ^ flip) for i in range(size)])  145 us
    ppermute x88, starting transfers between devices, swap(): return lax.ppermute(values, name, [(i, i ^ flip) for i in range(size)])  66.9 us
    all_to_all x4, starting transfers between devices, to_ranks(): return lax.all_to_all(parts_in, ('z', 'c'), 0, 0, tiled=True)  13.7 us
    pallas_call x10, Pallas kernels, chip_call(): pl.pallas_call(kernel, in_specs=[SCALAR] * len(scalars) + [WHOLE] * len(a...  13.7 us
    unnamed x141, local copies, waits for them, and re-layouts  10.4 us
    dot_general x13, matrix products, matmul(): return jnp.dot(first_mat, second_mat, preferred_element_type=f32)  9.58 us
    dot_general x16, matrix products, transposed_product(): lax.dot_general(first_mat, second_mat, (((1,), (1,)), ((), ())), preferre...  8.76 us
    dot_general x8, matrix products, outer_product_sum(): lax.dot_general(first_mat, second_mat, (((0,), (0,)), ((), ())), preferre...  8.47 us
  transfers between devices with their start and end apart: 94, of which 43 were waited for; matrix products, arithmetic and copies ran while one was open for 17% of the time, Pallas kernels for 6%

profile of v1, /device:TPU:0, one launch (start us, length us, event | category | flops | bytes accessed | tf_op | source)
XLA Modules:
  0.0 352.0 jit_solution(11739772987814752145)
XLA Ops:
  8.2 4.1 %collective-permute-start = (bf16[64,1024]{1,0:T(8,128)(2,1)S(1)}, bf16[64,1024]{1,0:T(8,128)(2,1)S(1)}, u32[]{:S(2)}, u32[]{:S(2)}) collective-permute-start(bf16[64,1024]{1,0:T(8,128)(2,1)S(1)} %get-tuple-element.320), channel_id=1, source_target_pairs={{0,4},{4,0},{1,5},{5,1},{2,6},{6,2},{3,7},{7,3},{8,12},{12,8},{9,1... | collective-permute-start | bytes 393224 | tf_op jit(solution)/shard_map/ppermute | solution.py:250
  12.3 1.9 lay_out.1
  14.2 3.4 all-to-all-start
  23.0 2.0 collective-permute-start.3
  26.0 3.5 all-to-all-start.2
  29.5 8.8 %collective-permute-done.1 = bf16[128,1024]{1,0:T(8,128)(2,1)S(1)} collective-permute-done((bf16[128,1024]{1,0:T(8,128)(2,1)S(1)}, bf16[128,1024]{1,0:T(8,128)(2,1)S(1)}, u32[]{:S(2)}, u32[]{:S(2)}) %collective-permute-start.1) | collective-permute-done | bytes 262176 | tf_op jit(solution)/shard_map/ppermute | solution.py:250
  44.9 2.3 collective-permute-start.19
  53.3 2.4 collective-permute-start.9
  55.7 3.2 all-to-all-start.1
  60.3 8.4 %all-to-all-done.1 = bf16[32,6,32]{2,1,0:T(8,128)(2,1)S(1)} async-done(((bf16[32,6,32]{2,1,0:T(8,128)(2,1)}), bf16[32,6,32]{2,1,0:T(8,128)(2,1)S(1)}, u32[]{:S(2)}, u32[]{:S(2)}) %all-to-all-start.1) | async-done | bytes 12320 | tf_op jit(solution)/shard_map/all_to_all | solution.py:591
  70.9 2.5 collective-permute-start.12
  77.3 1.9 convolution_convert_fusion.9
  79.3 1.9 convolution_convert_fusion.10.v_ref
  81.1 5.6 %collective-permute-done.15.refs_3_ = bf16[2,4,32,256]{3,2,1,0:T(8,128)(2,1)S(1)} collective-permute-done((bf16[2,4,32,256]{3,2,1,0:T(8,128)(2,1)S(1)}, bf16[2,4,32,256]{3,2,1,0:T(8,128)(2,1)S(1)}, u32[]{:S(2)}, u32[]{:S(2)}) %collective-permute-start.15) | collective-permute-done | bytes 131104 | tf_op jit(solution)/shard_map/ppermute | solution.py:250
  86.8 2.2 attend.3
  94.5 6.4 %collective-permute-done.21 = bf16[128,1024]{1,0:T(8,128)(2,1)S(1)} collective-permute-done((bf16[128,1024]{1,0:T(8,128)(2,1)S(1)}, bf16[128,1024]{1,0:T(8,128)(2,1)S(1)}, u32[]{:S(2)}, u32[]{:S(2)}) %collective-permute-start.21) | collective-permute-done | bytes 262176 | tf_op jit(solution)/shard_map/ppermute | solution.py:250
  103.9 6.7 %collective-permute-done.18.came = bf16[128,1024]{1,0:T(8,128)(2,1)S(1)} collective-permute-done((bf16[128,1024]{1,0:T(8,128)(2,1)S(1)}, bf16[128,1024]{1,0:T(8,128)(2,1)S(1)}, u32[]{:S(2)}, u32[]{:S(2)}) %collective-permute-start.18) | collective-permute-done | bytes 262176 | tf_op jit(solution)/shard_map/ppermute | solution.py:250
  112.1 4.2 %collective-permute-done.25 = bf16[2,2,128,512]{3,2,1,0:T(8,128)(2,1)S(1)} collective-permute-done((bf16[2,2,128,512]{3,2,1,0:T(8,128)(2,1)S(1)}, bf16[2,2,128,512]{3,2,1,0:T(8,128)(2,1)S(1)}, u32[]{:S(2)}, u32[]{:S(2)}) %collective-permute-start.25) | collective-permute-done | bytes 524320 | tf_op jit(solution)/shard_map/ppermute | solution.py:250
  116.3 2.0 collective-permute-start.37
  121.5 3.3 collective-permute-done.37
  124.7 2.8 collective-permute-done.31.refs_3_
  128.2 2.1 collective-permute-done.30.refs_2_
  140.9 7.1 %collective-permute-done.36.came = bf16[128,1024]{1,0:T(8,128)(2,1)S(1)} collective-permute-done((bf16[128,1024]{1,0:T(8,128)(2,1)S(1)}, bf16[128,1024]{1,0:T(8,128)(2,1)S(1)}, u32[]{:S(2)}, u32[]{:S(2)}) %collective-permute-start.36) | collective-permute-done | bytes 262176 | tf_op jit(solution)/shard_map/ppermute | solution.py:250
  149.9 6.6 %collective-permute-done.42 = bf16[128,1024]{1,0:T(8,128)(2,1)S(1)} collective-permute-done((bf16[128,1024]{1,0:T(8,128)(2,1)S(1)}, bf16[128,1024]{1,0:T(8,128)(2,1)S(1)}, u32[]{:S(2)}, u32[]{:S(2)}) %collective-permute-start.42) | collective-permute-done | bytes 262176 | tf_op jit(solution)/shard_map/ppermute | solution.py:250
  164.2 6.9 %collective-permute-done.45.came = bf16[128,1024]{1,0:T(8,128)(2,1)S(1)} collective-permute-done((bf16[128,1024]{1,0:T(8,128)(2,1)S(1)}, bf16[128,1024]{1,0:T(8,128)(2,1)S(1)}, u32[]{:S(2)}, u32[]{:S(2)}) %collective-permute-start.45) | collective-permute-done | bytes 262176 | tf_op jit(solution)/shard_map/ppermute | solution.py:250
  175.4 6.4 %collective-permute-done.48 = bf16[128,1024]{1,0:T(8,128)(2,1)S(1)} collective-permute-done((bf16[128,1024]{1,0:T(8,128)(2,1)S(1)}, bf16[128,1024]{1,0:T(8,128)(2,1)S(1)}, u32[]{:S(2)}, u32[]{:S(2)}) %collective-permute-start.48) | collective-permute-done | bytes 262176 | tf_op jit(solution)/shard_map/ppermute | solution.py:250
  189.0 2.4 pad_maximum_fusion
  191.5 4.6 %collective-permute-done.51.refs_2_ = bf16[128,1024]{1,0:T(8,128)(2,1)S(1)} collective-permute-done((bf16[128,1024]{1,0:T(8,128)(2,1)S(1)}, bf16[128,1024]{1,0:T(8,128)(2,1)S(1)}, u32[]{:S(2)}, u32[]{:S(2)}) %collective-permute-start.51) | collective-permute-done | bytes 262176 | tf_op jit(solution)/shard_map/ppermute | solution.py:250
  196.9 1.8 norm_back.2
  203.3 6.0 %collective-permute-done.58 = bf16[64,1024]{1,0:T(8,128)(2,1)S(1)} collective-permute-done((bf16[64,1024]{1,0:T(8,128)(2,1)S(1)}, bf16[64,1024]{1,0:T(8,128)(2,1)S(1)}, u32[]{:S(2)}, u32[]{:S(2)}) %collective-permute-start.58) | collective-permute-done | bytes 131104 | tf_op jit(solution)/shard_map/ppermute | solution.py:250
  214.5 2.0 attend_back.5
  220.2 6.8 %collective-permute-done.57.refs_2_ = bf16[128,1024]{1,0:T(8,128)(2,1)S(1)} collective-permute-done((bf16[128,1024]{1,0:T(8,128)(2,1)S(1)}, bf16[128,1024]{1,0:T(8,128)(2,1)S(1)}, u32[]{:S(2)}, u32[]{:S(2)}) %collective-permute-start.57) | collective-permute-done | bytes 262176 | tf_op jit(solution)/shard_map/ppermute | solution.py:250
  235.5 1.9 collective-permute-done.63
  237.4 1.8 collective-permute-start.68
  242.7 2.0 attend_back.7
  246.5 2.0 convolution_convert_fusion.3
  254.6 3.1 collective-permute-done.65.refs_3_
  262.7 2.5 collective-permute-start.84
  269.8 18.6 %collective-permute-done.84 = bf16[2,128,1024]{2,1,0:T(8,128)(2,1)S(1)} collective-permute-done((bf16[2,128,1024]{2,1,0:T(8,128)(2,1)S(1)}, bf16[2,128,1024]{2,1,0:T(8,128)(2,1)S(1)}, u32[]{:S(2)}, u32[]{:S(2)}) %collective-permute-start.84) | collective-permute-done | bytes 524320 | tf_op jit(solution)/shard_map/ppermute | solution.py:250
  289.6 2.2 collective-permute-done.71
  295.3 2.1 collective-permute-start.79
  299.4 5.5 %collective-permute-done.78 = bf16[64,1024]{1,0:T(8,128)(2,1)S(1)} collective-permute-done((bf16[64,1024]{1,0:T(8,128)(2,1)S(1)}, bf16[64,1024]{1,0:T(8,128)(2,1)S(1)}, u32[]{:S(2)}, u32[]{:S(2)}) %collective-permute-start.78) | collective-permute-done | bytes 131104 | tf_op jit(solution)/shard_map/ppermute | solution.py:250
  311.4 2.0 collective-permute-start.83
  313.4 3.4 all-to-all-start.4
  317.9 8.8 %collective-permute-done.81 = bf16[128,1024]{1,0:T(8,128)(2,1)S(1)} collective-permute-done((bf16[128,1024]{1,0:T(8,128)(2,1)S(1)}, bf16[128,1024]{1,0:T(8,128)(2,1)S(1)}, u32[]{:S(2)}, u32[]{:S(2)}) %collective-permute-start.81) | collective-permute-done | bytes 262176 | tf_op jit(solution)/shard_map/ppermute | solution.py:250
  326.8 5.5 %collective-permute-done.83 = bf16[128,1024]{1,0:T(8,128)(2,1)S(1)} collective-permute-done((bf16[128,1024]{1,0:T(8,128)(2,1)S(1)}, bf16[128,1024]{1,0:T(8,128)(2,1)S(1)}, u32[]{:S(2)}, u32[]{:S(2)}) %collective-permute-start.83) | collective-permute-done | bytes 262176 | tf_op jit(solution)/shard_map/ppermute | solution.py:250
  333.2 3.5 all-to-all-start.3
  340.4 3.6 %all-to-all-done.3.in_ref = bf16[4,32,1536]{2,1,0:T(8,128)(2,1)S(1)} async-done(((bf16[4,32,1536]{2,1,0:T(8,128)(2,1)}), bf16[4,32,1536]{2,1,0:T(8,128)(2,1)S(1)}, u32[]{:S(2)}, u32[]{:S(2)}) %all-to-all-start.3) | async-done | bytes 393248 | tf_op jit(solution)/shard_map/all_to_all | solution.py:546
  (493 shorter events, 134.4 us)
Async XLA Ops:
  8.2 14.6 %collective-permute-start = (bf16[64,1024]{1,0:T(8,128)(2,1)S(1)}, bf16[64,1024]{1,0:T(8,128)(2,1)S(1)}, u32[]{:S(2)}, u32[]{:S(2)}) collective-permute-start(bf16[64,1024]{1,0:T(8,128)(2,1)S(1)} %get-tuple-element.320), channel_id=1, source_target_pairs={{0,4},{4,0},{1,5},{5,1},{2,6},{6,2},{3,7},{7,3},{8,12},{12,8},{9,1... | collective-permute-start | bytes 393224 | tf_op jit(solution)/shard_map/ppermute | solution.py:250
  22.9 15.4 %collective-permute-start.1 = (bf16[128,1024]{1,0:T(8,128)(2,1)S(1)}, bf16[128,1024]{1,0:T(8,128)(2,1)S(1)}, u32[]{:S(2)}, u32[]{:S(2)}) collective-permute-start(bf16[128,1024]{1,0:T(8,128)(2,1)S(1)} %bitcast.343), channel_id=1, source_target_pairs={{0,4},{4,0},{1,5},{5,1},{2,6},{6,2},{3,7},{7,3},{8,12},{12,8},{9,1... | collective-permute-start | bytes 786440 | tf_op jit(solution)/shard_map/ppermute | solution.py:250
  23.0 15.3 %collective-permute-start.3 = (bf16[128,1024]{1,0:T(8,128)(2,1)S(1)}, bf16[128,1024]{1,0:T(8,128)(2,1)S(1)}, u32[]{:S(2)}, u32[]{:S(2)}) collective-permute-start(bf16[128,1024]{1,0:T(8,128)(2,1)S(1)} %pad_maximum_fusion.11.res), channel_id=1, source_target_pairs={{0,2},{2,0},{1,3},{3,1},{4,6},{6,4},{5,7},{7,5},{8,10},{10,8},{9,1... | collective-permute-start | bytes 786440 | tf_op jit(solution)/shard_map/ppermute | solution.py:250
  25.2 13.3 %collective-permute-start.2 = (bf16[128,1024]{1,0:T(8,128)(2,1)S(1)}, bf16[128,1024]{1,0:T(8,128)(2,1)S(1)}, u32[]{:S(2)}, u32[]{:S(2)}) collective-permute-start(bf16[128,1024]{1,0:T(8,128)(2,1)S(1)} %pad_maximum_fusion.11.res), channel_id=1, source_target_pairs={{0,1},{1,0},{2,3},{3,2},{4,5},{5,4},{6,7},{7,6},{8,9},{9,8},{10,11... | collective-permute-start | bytes 786440 | tf_op jit(solution)/shard_map/ppermute | solution.py:250
  26.0 25.7 %all-to-all-start.2 = ((bf16[4,32,1792]{2,1,0:T(8,128)(2,1)}), bf16[4,32,1792]{2,1,0:T(8,128)(2,1)S(1)}, u32[]{:S(2)}, u32[]{:S(2)}) async-start(bf16[4,32,1792]{2,1,0:T(8,128)(2,1)} %pad_maximum_fusion.9), calls=%async_computation.2 | async-start | bytes 917504 | tf_op jit(solution)/shard_map/all_to_all | solution.py:546
  44.9 10.9 %collective-permute-start.19 = (bf16[64,1024]{1,0:T(8,128)(2,1)S(1)}, bf16[64,1024]{1,0:T(8,128)(2,1)S(1)}, u32[]{:S(2)}, u32[]{:S(2)}) collective-permute-start(bf16[64,1024]{1,0:T(8,128)(2,1)S(1)} %get-tuple-element.318), channel_id=1, source_target_pairs={{0,4},{4,0},{1,5},{5,1},{2,6},{6,2},{3,7},{7,3},{8,12},{12,8},{9,1... | collective-permute-start | bytes 393224 | tf_op jit(solution)/shard_map/ppermute | solution.py:250
  50.4 18.5 %collective-permute-start.7 = (bf16[2,2,128,512]{3,2,1,0:T(8,128)(2,1)S(1)}, bf16[2,2,128,512]{3,2,1,0:T(8,128)(2,1)S(1)}, u32[]{:S(2)}, u32[]{:S(2)}) collective-permute-start(bf16[2,2,128,512]{3,2,1,0:T(8,128)(2,1)S(1)} %maximum_select_fusion.9), channel_id=1, source_target_pairs={{0,16},{8,24},{16,0},{24,8},{1,17},{9,25},{17,1},{25,9},{2,18},{10... | collective-permute-start | bytes 1572872 | tf_op jit(solution)/shard_map/ppermute | solution.py:250
  51.7 17.3 %collective-permute-start.8 = (bf16[2,2,128,512]{3,2,1,0:T(8,128)(2,1)S(1)}, bf16[2,2,128,512]{3,2,1,0:T(8,128)(2,1)}, u32[]{:S(2)}, u32[]{:S(2)}) collective-permute-start(bf16[2,2,128,512]{3,2,1,0:T(8,128)(2,1)S(1)} %maximum_select_fusion.10), channel_id=1, source_target_pairs={{0,8},{8,0},{16,24},{24,16},{1,9},{9,1},{17,25},{25,17},{2,10},{10... | collective-permute-start | bytes 1572872 | tf_op jit(solution)/shard_map/ppermute | solution.py:250
  53.3 17.6 %collective-permute-start.9 = (bf16[128,1024]{1,0:T(8,128)(2,1)S(1)}, bf16[128,1024]{1,0:T(8,128)(2,1)S(1)}, u32[]{:S(2)}, u32[]{:S(2)}) collective-permute-start(bf16[128,1024]{1,0:T(8,128)(2,1)S(1)} %bitcast.333), channel_id=1, source_target_pairs={{0,4},{4,0},{1,5},{5,1},{2,6},{6,2},{3,7},{7,3},{8,12},{12,8},{9,1... | collective-permute-start | bytes 786440 | tf_op jit(solution)/shard_map/ppermute | solution.py:250
  55.7 13.0 %all-to-all-start.1 = ((bf16[32,6,32]{2,1,0:T(8,128)(2,1)}), bf16[32,6,32]{2,1,0:T(8,128)(2,1)S(1)}, u32[]{:S(2)}, u32[]{:S(2)}) async-start(bf16[32,6,32]{2,1,0:T(8,128)(2,1)} %broadcast_in_dim.18), calls=%async_computation.1 | async-start | bytes 131072 | tf_op jit(solution)/shard_map/all_to_all | solution.py:591
  59.0 201.6 %reduce-scatter.2.cloned.1.call-start = ((), (), s32[]{:S(2)}) async-start(), calls=%async_computation.6 | async-start | bytes 5242880 | tf_op jit(solution)/shard_map/reduce_scatter | solution.py:704
  70.9 18.8 %collective-permute-start.12 = (bf16[128,1024]{1,0:T(8,128)(2,1)S(1)}, bf16[128,1024]{1,0:T(8,128)(2,1)S(1)}, u32[]{:S(2)}, u32[]{:S(2)}) collective-permute-start(bf16[128,1024]{1,0:T(8,128)(2,1)S(1)} %bitcast.318), channel_id=1, source_target_pairs={{0,4},{4,0},{1,5},{5,1},{2,6},{6,2},{3,7},{7,3},{8,12},{12,8},{9,1... | collective-permute-start | bytes 786440 | tf_op jit(solution)/shard_map/ppermute | solution.py:250
  73.6 17.7 %collective-permute-start.11 = (bf16[2,128,512]{2,1,0:T(8,128)(2,1)S(1)}, bf16[2,128,512]{2,1,0:T(8,128)(2,1)S(1)}, u32[]{:S(2)}, u32[]{:S(2)}) collective-permute-start(bf16[2,128,512]{2,1,0:T(8,128)(2,1)S(1)} %get-tuple-element.291), channel_id=1, source_target_pairs={{0,16},{8,24},{16,0},{24,8},{1,17},{9,25},{17,1},{25,9},{2,18},{10... | collective-permute-start | bytes 786440 | tf_op jit(solution)/shard_map/ppermute | solution.py:250
  74.3 17.2 %collective-permute-start.10 = (bf16[2,128,512]{2,1,0:T(8,128)(2,1)S(1)}, bf16[2,128,512]{2,1,0:T(8,128)(2,1)S(1)}, u32[]{:S(2)}, u32[]{:S(2)}) collective-permute-start(bf16[2,128,512]{2,1,0:T(8,128)(2,1)S(1)} %get-tuple-element.294), channel_id=1, source_target_pairs={{0,8},{8,0},{16,24},{24,16},{1,9},{9,1},{17,25},{25,17},{2,10},{10... | collective-permute-start | bytes 786440 | tf_op jit(solution)/shard_map/ppermute | solution.py:250
  75.8 10.9 %collective-permute-start.15 = (bf16[2,4,32,256]{3,2,1,0:T(8,128)(2,1)S(1)}, bf16[2,4,32,256]{3,2,1,0:T(8,128)(2,1)S(1)}, u32[]{:S(2)}, u32[]{:S(2)}) collective-permute-start(bf16[2,4,32,256]{3,2,1,0:T(8,128)(2,1)S(1)} %get-tuple-element.287), channel_id=1, source_target_pairs={{0,3},{1,2},{2,1},{3,0},{4,7},{5,6},{6,5},{7,4},{8,11},{9,10},{10,... | collective-permute-start | bytes 393224 | tf_op jit(solution)/shard_map/ppermute | solution.py:250
  76.1 13.2 %collective-permute-start.14 = (bf16[2,4,32,256]{3,2,1,0:T(8,128)(2,1)S(1)}, bf16[2,4,32,256]{3,2,1,0:T(8,128)(2,1)S(1)}, u32[]{:S(2)}, u32[]{:S(2)}) collective-permute-start(bf16[2,4,32,256]{3,2,1,0:T(8,128)(2,1)S(1)} %get-tuple-element.288), channel_id=1, source_target_pairs={{0,2},{1,3},{2,0},{3,1},{4,6},{5,7},{6,4},{7,5},{8,10},{9,11},{10,... | collective-permute-start | bytes 393224 | tf_op jit(solution)/shard_map/ppermute | solution.py:250
  89.2 11.6 %collective-permute-start.21 = (bf16[128,1024]{1,0:T(8,128)(2,1)S(1)}, bf16[128,1024]{1,0:T(8,128)(2,1)S(1)}, u32[]{:S(2)}, u32[]{:S(2)}) collective-permute-start(bf16[128,1024]{1,0:T(8,128)(2,1)S(1)} %pad_maximum_fusion.13), channel_id=1, source_target_pairs={{0,2},{2,0},{1,3},{3,1},{4,6},{6,4},{5,7},{7,5},{8,10},{10,8},{9,1... | collective-permute-start | bytes 786440 | tf_op jit(solution)/shard_map/ppermute | solution.py:250
  89.8 20.8 %collective-permute-start.23 = (bf16[128,1024]{1,0:T(8,128)(2,1)S(1)}, bf16[128,1024]{1,0:T(8,128)(2,1)S(1)}, u32[]{:S(2)}, u32[]{:S(2)}) collective-permute-start(bf16[128,1024]{1,0:T(8,128)(2,1)S(1)} %copy-done.51), channel_id=1, source_target_pairs={{0,4},{4,0},{1,5},{5,1},{2,6},{6,2},{3,7},{7,3},{8,12},{12,8},{9,1... | collective-permute-start | bytes 786440 | tf_op jit(solution)/shard_map/ppermute | solution.py:250
  91.6 29.8 %collective-permute-start.32 = (bf16[2,128,1024]{2,1,0:T(8,128)(2,1)S(1)}, bf16[2,128,1024]{2,1,0:T(8,128)(2,1)S(1)}, u32[]{:S(2)}, u32[]{:S(2)}) collective-permute-start(bf16[2,128,1024]{2,1,0:T(8,128)(2,1)S(1)} %maximum_select_fusion.14), channel_id=1, source_target_pairs={{0,8},{8,0},{16,24},{24,16},{1,9},{9,1},{17,25},{25,17},{2,10},{10... | collective-permute-start | bytes 1572872 | tf_op jit(solution)/shard_map/ppermute | solution.py:250
  101.0 15.3 %collective-permute-start.25 = (bf16[2,2,128,512]{3,2,1,0:T(8,128)(2,1)S(1)}, bf16[2,2,128,512]{3,2,1,0:T(8,128)(2,1)S(1)}, u32[]{:S(2)}, u32[]{:S(2)}) collective-permute-start(bf16[2,2,128,512]{3,2,1,0:T(8,128)(2,1)S(1)} %maximum_select_fusion.13), channel_id=1, source_target_pairs={{0,8},{8,0},{16,24},{24,16},{1,9},{9,1},{17,25},{25,17},{2,10},{10... | collective-permute-start | bytes 1572872 | tf_op jit(solution)/shard_map/ppermute | solution.py:250
  102.4 16.2 %collective-permute-start.28 = (bf16[2,2,128,512]{3,2,1,0:T(8,128)(2,1)S(1)}, bf16[2,2,128,512]{3,2,1,0:T(8,128)(2,1)S(1)}, u32[]{:S(2)}, u32[]{:S(2)}) collective-permute-start(bf16[2,2,128,512]{3,2,1,0:T(8,128)(2,1)S(1)} %maximum_select_fusion.12), channel_id=1, source_target_pairs={{0,16},{8,24},{16,0},{24,8},{1,17},{9,25},{17,1},{25,9},{2,18},{10... | collective-permute-start | bytes 1572872 | tf_op jit(solution)/shard_map/ppermute | solution.py:250
  110.9 16.7 %collective-permute-start.26 = (bf16[128,1024]{1,0:T(8,128)(2,1)S(1)}, bf16[128,1024]{1,0:T(8,128)(2,1)S(1)}, u32[]{:S(2)}, u32[]{:S(2)}) collective-permute-start(bf16[128,1024]{1,0:T(8,128)(2,1)S(1)} %get-tuple-element.172.res), channel_id=1, source_target_pairs={{0,2},{2,0},{1,3},{3,1},{4,6},{6,4},{5,7},{7,5},{8,10},{10,8},{9,1... | collective-permute-start | bytes 786440 | tf_op jit(solution)/shard_map/ppermute | solution.py:250
  111.0 20.3 %collective-permute-start.24 = (bf16[128,1024]{1,0:T(8,128)(2,1)S(1)}, bf16[128,1024]{1,0:T(8,128)(2,1)S(1)}, u32[]{:S(2)}, u32[]{:S(2)}) collective-permute-start(bf16[128,1024]{1,0:T(8,128)(2,1)S(1)} %get-tuple-element.172.res), channel_id=1, source_target_pairs={{0,1},{1,0},{2,3},{3,2},{4,5},{5,4},{6,7},{7,6},{8,9},{9,8},{10,11... | collective-permute-start | bytes 786440 | tf_op jit(solution)/shard_map/ppermute | solution.py:250
  118.7 13.3 %collective-permute-start.33 = (bf16[2,128,1024]{2,1,0:T(8,128)(2,1)S(1)}, bf16[2,128,1024]{2,1,0:T(8,128)(2,1)S(1)}, u32[]{:S(2)}, u32[]{:S(2)}) collective-permute-start(bf16[2,128,1024]{2,1,0:T(8,128)(2,1)S(1)} %maximum_select_fusion.16), channel_id=1, source_target_pairs={{0,16},{8,24},{16,0},{24,8},{1,17},{9,25},{17,1},{25,9},{2,18},{10... | collective-permute-start | bytes 1572872 | tf_op jit(solution)/shard_map/ppermute | solution.py:250
  132.5 25.8 %collective-permute-start.39 = (bf16[2,2,128,1024]{3,2,1,0:T(8,128)(2,1)S(1)}, bf16[2,2,128,1024]{3,2,1,0:T(8,128)(2,1)S(1)}, u32[]{:S(2)}, u32[]{:S(2)}) collective-permute-start(bf16[2,2,128,1024]{3,2,1,0:T(8,128)(2,1)S(1)} %maximum_select_fusion.6), channel_id=1, source_target_pairs={{0,16},{8,24},{16,0},{24,8},{1,17},{9,25},{17,1},{25,9},{2,18},{10... | collective-permute-start | bytes 3145736 | tf_op jit(solution)/shard_map/ppermute | solution.py:250
  134.0 23.8 %collective-permute-start.40 = (bf16[2,2,128,1024]{3,2,1,0:T(8,128)(2,1)S(1)}, bf16[2,2,128,1024]{3,2,1,0:T(8,128)(2,1)S(1)}, u32[]{:S(2)}, u32[]{:S(2)}) collective-permute-start(bf16[2,2,128,1024]{3,2,1,0:T(8,128)(2,1)S(1)} %maximum_select_fusion.7), channel_id=1, source_target_pairs={{0,8},{8,0},{16,24},{24,16},{1,9},{9,1},{17,25},{25,17},{2,10},{10... | collective-permute-start | bytes 3145736 | tf_op jit(solution)/shard_map/ppermute | solution.py:250
  149.9 10.5 %collective-permute-start.38 = (bf16[128,1024]{1,0:T(8,128)(2,1)S(1)}, bf16[128,1024]{1,0:T(8,128)(2,1)S(1)}, u32[]{:S(2)}, u32[]{:S(2)}) collective-permute-start(bf16[128,1024]{1,0:T(8,128)(2,1)S(1)} %get-tuple-element.188.res), channel_id=1, source_target_pairs={{0,1},{1,0},{2,3},{3,2},{4,5},{5,4},{6,7},{7,6},{8,9},{9,8},{10,11... | collective-permute-start | bytes 786440 | tf_op jit(solution)/shard_map/ppermute | solution.py:250
  198.8 10.7 %collective-permute-start.52 = (bf16[128,1024]{1,0:T(8,128)(2,1)S(1)}, bf16[128,1024]{1,0:T(8,128)(2,1)S(1)}, u32[]{:S(2)}, u32[]{:S(2)}) collective-permute-start(bf16[128,1024]{1,0:T(8,128)(2,1)S(1)} %get-tuple-element.206), channel_id=1, source_target_pairs={{0,1},{1,0},{2,3},{3,2},{4,5},{5,4},{6,7},{7,6},{8,9},{9,8},{10,11... | collective-permute-start | bytes 786440 | tf_op jit(solution)/shard_map/ppermute | solution.py:250
  201.4 11.1 %collective-permute-start.54 = (bf16[128,1024]{1,0:T(8,128)(2,1)S(1)}, bf16[128,1024]{1,0:T(8,128)(2,1)S(1)}, u32[]{:S(2)}, u32[]{:S(2)}) collective-permute-start(bf16[128,1024]{1,0:T(8,128)(2,1)S(1)} %get-tuple-element.206), channel_id=1, source_target_pairs={{0,2},{2,0},{1,3},{3,1},{4,6},{6,4},{5,7},{7,5},{8,10},{10,8},{9,1... | collective-permute-start | bytes 786440 | tf_op jit(solution)/shard_map/ppermute | solution.py:250
  228.7 10.5 %collective-permute-start.60 = (bf16[128,1024]{1,0:T(8,128)(2,1)S(1)}, bf16[128,1024]{1,0:T(8,128)(2,1)S(1)}, u32[]{:S(2)}, u32[]{:S(2)}) collective-permute-start(bf16[128,1024]{1,0:T(8,128)(2,1)S(1)} %get-tuple-element.224), channel_id=1, source_target_pairs={{0,2},{2,0},{1,3},{3,1},{4,6},{6,4},{5,7},{7,5},{8,10},{10,8},{9,1... | collective-permute-start | bytes 786440 | tf_op jit(solution)/shard_map/ppermute | solution.py:250
  229.0 10.3 %collective-permute-start.59 = (bf16[128,1024]{1,0:T(8,128)(2,1)S(1)}, bf16[128,1024]{1,0:T(8,128)(2,1)S(1)}, u32[]{:S(2)}, u32[]{:S(2)}) collective-permute-start(bf16[128,1024]{1,0:T(8,128)(2,1)S(1)} %get-tuple-element.224), channel_id=1, source_target_pairs={{0,1},{1,0},{2,3},{3,2},{4,5},{5,4},{6,7},{7,6},{8,9},{9,8},{10,11... | collective-permute-start | bytes 786440 | tf_op jit(solution)/shard_map/ppermute | solution.py:250
  234.7 14.4 %collective-permute-start.69 = (bf16[2,32,1024]{2,1,0:T(8,128)(2,1)S(1)}, bf16[2,32,1024]{2,1,0:T(8,128)(2,1)S(1)}, u32[]{:S(2)}, u32[]{:S(2)}) collective-permute-start(bf16[2,32,1024]{2,1,0:T(8,128)(2,1)S(1)} %get-tuple-element.271), channel_id=1, source_target_pairs={{0,3},{1,2},{2,1},{3,0},{4,7},{5,6},{6,5},{7,4},{8,11},{9,10},{10,... | collective-permute-start | bytes 393224 | tf_op jit(solution)/shard_map/ppermute | solution.py:250
  237.4 15.8 %collective-permute-start.68 = (bf16[2,32,1024]{2,1,0:T(8,128)(2,1)S(1)}, bf16[2,32,1024]{2,1,0:T(8,128)(2,1)S(1)}, u32[]{:S(2)}, u32[]{:S(2)}) collective-permute-start(bf16[2,32,1024]{2,1,0:T(8,128)(2,1)S(1)} %get-tuple-element.272), channel_id=1, source_target_pairs={{0,2},{1,3},{2,0},{3,1},{4,6},{5,7},{6,4},{7,5},{8,10},{9,11},{10,... | collective-permute-start | bytes 393224 | tf_op jit(solution)/shard_map/ppermute | solution.py:250
  239.2 13.9 %collective-permute-start.67 = (bf16[2,32,1024]{2,1,0:T(8,128)(2,1)S(1)}, bf16[2,32,1024]{2,1,0:T(8,128)(2,1)S(1)}, u32[]{:S(2)}, u32[]{:S(2)}) collective-permute-start(bf16[2,32,1024]{2,1,0:T(8,128)(2,1)S(1)} %get-tuple-element.273), channel_id=1, source_target_pairs={{0,1},{1,0},{2,3},{3,2},{4,5},{5,4},{6,7},{7,6},{8,9},{9,8},{10,11... | collective-permute-start | bytes 393224 | tf_op jit(solution)/shard_map/ppermute | solution.py:250
  262.7 25.8 %collective-permute-start.84 = (bf16[2,128,1024]{2,1,0:T(8,128)(2,1)S(1)}, bf16[2,128,1024]{2,1,0:T(8,128)(2,1)S(1)}, u32[]{:S(2)}, u32[]{:S(2)}) collective-permute-start(bf16[2,128,1024]{2,1,0:T(8,128)(2,1)S(1)} %dynamic-slice_bitcast_fusion.2), channel_id=1, source_target_pairs={{0,4},{4,0},{1,5},{5,1},{2,6},{6,2},{3,7},{7,3},{8,12},{12,8},{9,1... | collective-permute-start | bytes 1572872 | tf_op jit(solution)/shard_map/ppermute | solution.py:250
  265.9 23.6 %collective-permute-start.72 = (bf16[128,1024]{1,0:T(8,128)(2,1)S(1)}, bf16[128,1024]{1,0:T(8,128)(2,1)S(1)}, u32[]{:S(2)}, u32[]{:S(2)}) collective-permute-start(bf16[128,1024]{1,0:T(8,128)(2,1)S(1)} %slice.445), channel_id=1, source_target_pairs={{0,1},{1,0},{2,3},{3,2},{4,5},{5,4},{6,7},{7,6},{8,9},{9,8},{10,11... | collective-permute-start | bytes 786440 | tf_op jit(solution)/shard_map/ppermute | solution.py:250
  267.2 24.7 %collective-permute-start.71 = (bf16[2,2,128,1024]{3,2,1,0:T(8,128)(2,1)S(1)}, bf16[2,2,128,1024]{3,2,1,0:T(8,128)(2,1)S(1)}, u32[]{:S(2)}, u32[]{:S(2)}) collective-permute-start(bf16[2,2,128,1024]{3,2,1,0:T(8,128)(2,1)S(1)} %dynamic-slice_bitcast_fusion), channel_id=1, source_target_pairs={{0,16},{8,24},{16,0},{24,8},{1,17},{9,25},{17,1},{25,9},{2,18},{10... | collective-permute-start | bytes 3145736 | tf_op jit(solution)/shard_map/ppermute | solution.py:250
  268.5 24.3 %collective-permute-start.70 = (bf16[2,2,128,1024]{3,2,1,0:T(8,128)(2,1)S(1)}, bf16[2,2,128,1024]{3,2,1,0:T(8,128)(2,1)S(1)}, u32[]{:S(2)}, u32[]{:S(2)}) collective-permute-start(bf16[2,2,128,1024]{3,2,1,0:T(8,128)(2,1)S(1)} %dynamic-slice_bitcast_fusion.1), channel_id=1, source_target_pairs={{0,8},{8,0},{16,24},{24,16},{1,9},{9,1},{17,25},{25,17},{2,10},{10... | collective-permute-start | bytes 3145736 | tf_op jit(solution)/shard_map/ppermute | solution.py:250
  269.4 20.1 %collective-permute-start.74 = (bf16[128,1024]{1,0:T(8,128)(2,1)S(1)}, bf16[128,1024]{1,0:T(8,128)(2,1)S(1)}, u32[]{:S(2)}, u32[]{:S(2)}) collective-permute-start(bf16[128,1024]{1,0:T(8,128)(2,1)S(1)} %fusion.52), channel_id=1, source_target_pairs={{0,2},{2,0},{1,3},{3,1},{4,6},{6,4},{5,7},{7,5},{8,10},{10,8},{9,1... | collective-permute-start | bytes 786440 | tf_op jit(solution)/shard_map/ppermute | solution.py:250
  293.3 11.6 %collective-permute-start.78 = (bf16[64,1024]{1,0:T(8,128)(2,1)S(1)}, bf16[64,1024]{1,0:T(8,128)(2,1)S(1)}, u32[]{:S(2)}, u32[]{:S(2)}) collective-permute-start(bf16[64,1024]{1,0:T(8,128)(2,1)S(1)} %get-tuple-element.309), channel_id=1, source_target_pairs={{0,4},{4,0},{1,5},{5,1},{2,6},{6,2},{3,7},{7,3},{8,12},{12,8},{9,1... | collective-permute-start | bytes 393224 | tf_op jit(solution)/shard_map/ppermute | solution.py:250
  294.6 12.0 %collective-permute-start.80 = (bf16[2,128,1024]{2,1,0:T(8,128)(2,1)S(1)}, bf16[2,128,1024]{2,1,0:T(8,128)(2,1)S(1)}, u32[]{:S(2)}, u32[]{:S(2)}) collective-permute-start(bf16[2,128,1024]{2,1,0:T(8,128)(2,1)S(1)} %dynamic-slice_bitcast_fusion.4), channel_id=1, source_target_pairs={{0,16},{8,24},{16,0},{24,8},{1,17},{9,25},{17,1},{25,9},{2,18},{10... | collective-permute-start | bytes 1572872 | tf_op jit(solution)/shard_map/ppermute | solution.py:250
  295.3 11.1 %collective-permute-start.79 = (bf16[64,1024]{1,0:T(8,128)(2,1)S(1)}, bf16[64,1024]{1,0:T(8,128)(2,1)S(1)}, u32[]{:S(2)}, u32[]{:S(2)}) collective-permute-start(bf16[64,1024]{1,0:T(8,128)(2,1)S(1)} %get-tuple-element.305), channel_id=1, source_target_pairs={{0,4},{4,0},{1,5},{5,1},{2,6},{6,2},{3,7},{7,3},{8,12},{12,8},{9,1... | collective-permute-start | bytes 393224 | tf_op jit(solution)/shard_map/ppermute | solution.py:250
  297.4 11.4 %collective-permute-start.82 = (bf16[2,128,1024]{2,1,0:T(8,128)(2,1)S(1)}, bf16[2,128,1024]{2,1,0:T(8,128)(2,1)S(1)}, u32[]{:S(2)}, u32[]{:S(2)}) collective-permute-start(bf16[2,128,1024]{2,1,0:T(8,128)(2,1)S(1)} %dynamic-slice_bitcast_fusion.3), channel_id=1, source_target_pairs={{0,8},{8,0},{16,24},{24,16},{1,9},{9,1},{17,25},{25,17},{2,10},{10... | collective-permute-start | bytes 1572872 | tf_op jit(solution)/shard_map/ppermute | solution.py:250
  306.9 19.8 %collective-permute-start.81 = (bf16[128,1024]{1,0:T(8,128)(2,1)S(1)}, bf16[128,1024]{1,0:T(8,128)(2,1)S(1)}, u32[]{:S(2)}, u32[]{:S(2)}) collective-permute-start(bf16[128,1024]{1,0:T(8,128)(2,1)S(1)} %dynamic-slice_bitcast_fusion.6), channel_id=1, source_target_pairs={{0,4},{4,0},{1,5},{5,1},{2,6},{6,2},{3,7},{7,3},{8,12},{12,8},{9,1... | collective-permute-start | bytes 786440 | tf_op jit(solution)/shard_map/ppermute | solution.py:250
  311.4 20.9 %collective-permute-start.83 = (bf16[128,1024]{1,0:T(8,128)(2,1)S(1)}, bf16[128,1024]{1,0:T(8,128)(2,1)S(1)}, u32[]{:S(2)}, u32[]{:S(2)}) collective-permute-start(bf16[128,1024]{1,0:T(8,128)(2,1)S(1)} %dynamic-slice_bitcast_fusion.5), channel_id=1, source_target_pairs={{0,4},{4,0},{1,5},{5,1},{2,6},{6,2},{3,7},{7,3},{8,12},{12,8},{9,1... | collective-permute-start | bytes 786440 | tf_op jit(solution)/shard_map/ppermute | solution.py:250
  313.4 19.8 %all-to-all-start.4 = ((bf16[4,32,1024]{2,1,0:T(8,128)(2,1)}), bf16[4,32,1024]{2,1,0:T(8,128)(2,1)S(1)}, u32[]{:S(2)}, u32[]{:S(2)}) async-start(bf16[4,32,1024]{2,1,0:T(8,128)(2,1)} %bitcast.128), calls=%async_computation.5 | async-start | bytes 524288 | tf_op jit(solution)/shard_map/all_to_all | solution.py:546
  316.8 20.5 %collective-permute-start.87 = (f32[6,1024]{1,0:T(8,128)S(1)}, f32[6,1024]{1,0:T(8,128)S(1)}, u32[]{:S(2)}, u32[]{:S(2)}) collective-permute-start(f32[6,1024]{1,0:T(8,128)S(1)} %add.297), channel_id=1, source_target_pairs={{0,4},{4,0},{1,5},{5,1},{2,6},{6,2},{3,7},{7,3},{8,12},{12,8},{9,1... | collective-permute-start | bytes 73736 | tf_op jit(solution)/shard_map/ppermute | solution.py:250
  333.2 10.9 %all-to-all-start.3 = ((bf16[4,32,1536]{2,1,0:T(8,128)(2,1)}), bf16[4,32,1536]{2,1,0:T(8,128)(2,1)S(1)}, u32[]{:S(2)}, u32[]{:S(2)}) async-start(bf16[4,32,1536]{2,1,0:T(8,128)(2,1)} %bitcast.119), calls=%async_computation.4 | async-start | bytes 786432 | tf_op jit(solution)/shard_map/all_to_all | solution.py:546
  (112 other events, 650.1 us)
Sparse Core Ops, SparseCore 0:
  196.9 51.7 reduce-scatter.1
